TPU v7x, 256 devices: a whole 4x4x8 slice. The times are simulated.
256 devices in a mesh: grp: 4 (over y), sub: 64 (over z, x, core).
Axes of the slice: x: 4, y: 4, z: 8, core: 2. Of those that a mesh axis runs over, the one named last changes fastest.
Arguments:
- neumann: bfloat16 [4, 64, 1024, 1024], P('grp', 'sub'), may hold values from -1 to 4
- dirichlet: bfloat16 [4, 64, 1024, 1024], P('grp', 'sub'), may hold values from -1 to 4
- coarse_inverse: float32 [4, 64, 128, 2048], P('grp', 'sub'), may hold values from -1 to 3
- loads: bfloat16 [4, 64, 1024, 256], P('grp', 'sub'), may hold values from -72 to 72
- iface_sizes: int32 [4, 64], P('grp', 'sub'), may hold values from 1 to 512, 16384 in all within a row
- wave_dirs: int32 [4, 64, 32], P('grp', 'sub'), may hold values from 0 to 63
Outputs:
- dual: float32 [4, 64, 512, 256], P('grp', 'sub')
- residual: float32 [4, 64, 512, 256], P('grp', 'sub')
Inputs may be any that keep to these rules, and one draw needn't show every extreme that they name: `iface_sizes`: the 64 sizes of one group sum to 16384, and in each group one size is exactly 512.
All inputs are finite; a program needn't handle non-finite values.
Results may differ from a plain program's by a relative error of at most 0.005.
Values may be sent and summed in bfloat16 or wider, within the bound.
No kernel may reach another device: no remote copies, remote signals or barrier semaphores. Data moves between devices by JAX's collectives and lax.ppermute only.
A program may use at most 64 MiB of HBM per device.

v0:
```python
import functools

import jax
import jax.numpy as jnp
from jax import lax
from jax.experimental import pallas as pl
from jax.experimental.pallas import tpu as pltpu
from jax.sharding import Mesh
from jax.sharding import PartitionSpec as P

NDIR = 64
ITERS = 2
WAVE_NUMBER = 0.785
SUB = ("z", "x", "c")
SPREAD = ("grp", "x", "c")
F32 = jnp.float32
BF16 = jnp.bfloat16
GRANT = pltpu.CompilerParams(vmem_limit_bytes=14 << 20)


def call(body, outs, flops=0, size=0):
    return pl.pallas_call(
        body,
        out_shape=[jax.ShapeDtypeStruct(shape, dtype) for shape, dtype in outs],
        compiler_params=GRANT,
        cost_estimate=pl.CostEstimate(flops=flops, bytes_accessed=size, transcendentals=0),
    )


def mm(a, b):
    return jnp.dot(a, b, preferred_element_type=F32)


def halves(value):
    high = value.astype(BF16)
    return high, (value - high.astype(F32)).astype(BF16)


def mm_wide(pair, value):
    high, low = halves(value)
    return mm(pair[0], high) + (mm(pair[0], low) + mm(pair[1], high))


def reversal(n):
    rows = lax.broadcasted_iota(jnp.int32, (n, n), 0)
    cols = lax.broadcasted_iota(jnp.int32, (n, n), 1)
    return (rows + cols == n - 1).astype(BF16)


def live_rows(size_ref, shape):
    return lax.broadcasted_iota(jnp.int32, shape, 0) < size_ref[0, 0]


def wave_parts(size, directions, reach):
    def basis(axis):
        def along(v):
            return v[:, None] if axis == 0 else v[None, :]

        def across(v):
            return v[None, :] if axis == 0 else v[:, None]

        rows = jnp.arange(reach).astype(F32)
        live = (jnp.arange(reach) < size).astype(F32)
        angle = 2.0 * jnp.pi * directions.astype(F32) / NDIR
        phase = (jnp.arange(directions.shape[0]) % 2).astype(F32) * (jnp.pi / 2.0)
        wave = jnp.cos(WAVE_NUMBER * along(rows) * across(jnp.cos(angle)) + across(phase))
        wave = wave * along(live) / jnp.sqrt(F32(reach))
        high = lax.reduce_precision(wave, 8, 7)
        return high.astype(BF16), (wave - high).astype(BF16)

    return basis(0), basis(1)


STEPS = 14


def exponent(value):
    return jnp.ceil(jnp.log2(jnp.maximum(value, 1e-30)))


def scale_of(power):
    return jnp.exp2(STEPS - power)


def side_by_side(rows):
    half = rows.shape[1] // 2
    return [rows[:, :half], rows[:, half:]]


def coded_sum(extra):
    power = exponent(jnp.abs(extra))
    value = extra * scale_of(power)
    first = jnp.round(value)
    rest = jnp.round((value - first) * 2.0**STEPS)
    return side_by_side(power) + side_by_side(first) + side_by_side(rest)


def pack(blocks, code, out_ref, copies):
    count, waves, columns = blocks.shape
    half = columns // 2
    power = exponent(jnp.max(jnp.abs(blocks), axis=1))
    scaled = jnp.round(blocks * scale_of(power)[:, None, :]).astype(jnp.int32).astype(jnp.int16)
    for k in range(count):
        tail = side_by_side(power[k : k + 1]) + code
        tail = jnp.concatenate(tail, axis=0).astype(jnp.int32).astype(jnp.int16)
        for i in copies[k]:
            out_ref[i, 0:waves] = scaled[k, :, :half]
            out_ref[i, waves : 2 * waves] = scaled[k, :, half:]
            out_ref[i, 2 * waves :] = tail


def no_sum(columns):
    return [jnp.zeros((1, columns // 2), F32)] * 6


def wide(value):
    return value.astype(jnp.int32).astype(F32)


def unpack(value, waves, extra):
    tail = wide(value[2 * waves :])
    back = 1.0 / scale_of(tail[0:4])
    rows = jnp.concatenate(
        [wide(value[0:waves]) * back[0:1], wide(value[waves : 2 * waves]) * back[1:2]], axis=1
    )
    if not extra:
        return rows, None
    sums = (tail[4:6] + tail[6:8] * 2.0**-STEPS) * back[2:4]
    return rows, jnp.concatenate([sums[0:1], sums[1:2]], axis=1)


def coded(value, out_ref):
    rows, columns = value.shape
    power = exponent(jnp.max(jnp.abs(value), axis=0, keepdims=True))
    out_ref[0:rows] = jnp.round(value * scale_of(power)).astype(jnp.int32).astype(jnp.int16)
    power = jnp.broadcast_to(power, (16, columns))
    out_ref[rows:] = power.astype(jnp.int32).astype(jnp.int16)


def decoded(ref):
    value = ref[...]
    rows = value.shape[0] - 16
    return wide(value[0:rows]) * (1.0 / scale_of(wide(value[rows:])[0:1]))


def heads_kernel(mat_ref, loads_ref, out_ref):
    reach = out_ref.shape[0] - 16
    coded(mm(mat_ref[0:reach], loads_ref[...]), out_ref)


def turn_kernel(mat_ref, own_ref, away_ref):
    reach = own_ref.shape[0]
    flip = reversal(reach)
    low = mm(flip, mat_ref[reach:]).astype(BF16)
    own_ref[:, 0:reach] = mm(low[:, reach:], flip).astype(BF16)
    own_ref[:, reach:] = low[:, :reach]
    away_ref[:, 0:reach] = mat_ref[0:reach, 0:reach]
    away_ref[:, reach:] = mm(mat_ref[0:reach, reach:], flip).astype(BF16)


def tile_kernel(near, far, tile_ref, out_ref):
    waves = tile_ref.shape[1] // (near * far)
    value = tile_ref[...]
    for j in range(near):
        pieces = [value[:, (k * near + j) * waves : (k * near + j + 1) * waves] for k in range(far)]
        coded(jnp.concatenate(pieces, axis=1), out_ref.at[j])


def parts_kernel(got_ref, out_ref):
    rows = out_ref.shape[1] // 2
    for j in range(got_ref.shape[0]):
        out_ref[j, 0:rows], out_ref[j, rows:] = halves(decoded(got_ref.at[j]))


def rhs_kernel(size_ref, mat_ref, loads_ref, heads_ref, wt_hi, wt_lo, rhs_ref, pay_ref):
    reach = rhs_ref.shape[0]
    low = mm(mat_ref[reach:], loads_ref[...])
    flip = reversal(reach)
    high_part = low.astype(BF16)
    rest = low - high_part.astype(F32)
    mid_part = rest.astype(BF16)
    low_part = (rest - mid_part.astype(F32)).astype(BF16)
    tails = mm(flip, high_part) + (mm(flip, mid_part) + mm(flip, low_part))
    rhs = jnp.where(live_rows(size_ref, tails.shape), tails - decoded(heads_ref), 0.0)
    rhs_ref[...] = rhs
    rows = mm_wide((wt_hi[...], wt_lo[...]), rhs)
    pack(rows[None], no_sum(rows.shape[1]), pay_ref, [range(pay_ref.shape[0])])


def inner_kernel(own_ref, away_ref, xr_ref, out_ref):
    reach = out_ref.shape[0]
    xr = xr_ref[...]
    out_ref[...] = mm(own_ref[:, 0:reach], xr) + mm(away_ref[:, 0:reach], xr)


def apply_kernel(mode, size_ref, own_ref, away_ref, inner_ref, x_ref, prev_ref, next_ref, wt_hi, wt_lo, *rest):
    reach = inner_ref.shape[0]
    outer = mm(own_ref[:, reach:], prev_ref[...]) + mm(away_ref[:, reach:], next_ref[...])
    product = inner_ref[...] - outer
    product = jnp.where(live_rows(size_ref, product.shape), product, 0.0)
    if mode == "start":
        rhs_ref, out_ref, pay_ref = rest
        product = rhs_ref[...] - product
        extra = None
    else:
        out_ref, pay_ref = rest
        extra = jnp.sum(x_ref[...] * product, axis=0, keepdims=True)
    out_ref[...] = product
    if mode == "last":
        half = extra.shape[1] // 2
        for i in range(pay_ref.shape[0]):
            pay_ref[i, 0:1] = extra[:, :half]
            pay_ref[i, 1:2] = extra[:, half:]
        return
    rows = mm_wide((wt_hi[...], wt_lo[...]), product)
    code = no_sum(rows.shape[1]) if extra is None else coded_sum(extra)
    pack(rows[None], code, pay_ref, [range(pay_ref.shape[0])])


def coarse_kernel(extra, groups, tiles_ref, got_ref, out_ref):
    near, twice, _ = tiles_ref.shape
    height = twice // 2
    waves = height // groups
    far = got_ref.shape[0]
    parts = [unpack(got_ref[k], waves, extra) for k in range(far)]
    stacked = jnp.concatenate([p[0] for p in parts], axis=0)
    if extra:
        code = coded_sum(sum([p[1] for p in parts[1:]], parts[0][1]))
    else:
        code = no_sum(stacked.shape[1])
    high, low = halves(stacked)
    for j in range(near):
        top = tiles_ref[j, 0:height]
        value = mm(top, high) + (mm(top, low) + mm(tiles_ref[j, height:], high))
        blocks = value.reshape(groups, waves, value.shape[1])
        pack(blocks, code, out_ref, [(h * near + j,) for h in range(groups)])


def summed(ref):
    total = ref[0]
    for i in range(1, ref.shape[0]):
        total = total + ref[i]
    return total


def gathered(ref, waves, extra):
    rows, row = unpack(ref[0], waves, extra)
    for i in range(1, ref.shape[0]):
        more, more_row = unpack(ref[i], waves, extra)
        rows = rows + more
        row = row + more_row if extra else None
    return rows, row


def lift(w_hi, w_lo, rows):
    return mm_wide((w_hi[...], w_lo[...]), rows)


def first_kernel(got_ref, w_hi, w_lo, dual_ref, dualr_ref):
    rows, _ = gathered(got_ref, w_hi.shape[1], False)
    dual = lift(w_hi, w_lo, rows)
    dual_ref[...] = dual
    dualr_ref[...] = dual.astype(BF16)


def project_kernel(got_ref, w_hi, w_lo, res_ref, rows_ref, out_ref, outr_ref):
    rows, _ = gathered(got_ref, w_hi.shape[1], False)
    rows_ref[...] = rows
    out = res_ref[...] - lift(w_hi, w_lo, rows)
    out_ref[...] = out
    outr_ref[...] = out.astype(BF16)


def search_kernel(first, got_ref, w_hi, w_lo, pre_ref, *rest):
    rows, rho = gathered(got_ref, w_hi.shape[1], True)
    out = pre_ref[...] - lift(w_hi, w_lo, rows)
    if first:
        rho_ref, out_ref, outr_ref = rest
    else:
        old_rho, old_dir, rho_ref, out_ref, outr_ref = rest
        out = out + rho / old_rho[0:1] * old_dir[...]
    rho_ref[...] = jnp.broadcast_to(rho, rho_ref.shape)
    out_ref[...] = out
    outr_ref[...] = out.astype(BF16)


def step_kernel(got_ref, w_hi, w_lo, rho_ref, dir_ref, img_ref, dual_ref, res_ref, rows_ref,
                new_dual, new_res, new_out, new_outr):
    rows, bottom = gathered(got_ref, w_hi.shape[1], True)
    alpha = rho_ref[0:1] / bottom
    new_dual[...] = dual_ref[...] + alpha * dir_ref[...]
    res = res_ref[...] - alpha * img_ref[...]
    new_res[...] = res
    out = res - lift(w_hi, w_lo, rows_ref[...] - alpha * rows)
    new_out[...] = out
    new_outr[...] = out.astype(BF16)


def partial_kernel(got_ref, out_ref):
    total = summed(got_ref)
    for i in range(out_ref.shape[0]):
        out_ref[i] = total


def final_kernel(got_ref, rho_ref, dir_ref, img_ref, dual_ref, res_ref, new_dual, new_res):
    total = summed(got_ref)
    bottom = jnp.concatenate([total[0:1], total[1:2]], axis=1)
    alpha = rho_ref[0:1] / bottom
    new_dual[...] = dual_ref[...] + alpha * dir_ref[...]
    new_res[...] = res_ref[...] - alpha * img_ref[...]


def passed_along(block, distance):
    n = lax.axis_size(SUB)
    return lax.ppermute(block, SUB, [((i - distance) % n, i) for i in range(n)])


def exchange(value, axes):
    return lax.all_to_all(value, axes, 0, 0, tiled=True)


def shards(neumann, dirichlet, coarse_inverse, loads, iface_sizes, wave_dirs):
    nmat, dmat = neumann[0, 0], dirichlet[0, 0]
    tile, load = coarse_inverse[0, 0], loads[0, 0]
    width, columns = load.shape
    reach = width // 2
    directions = wave_dirs[0, 0]
    waves = directions.shape[0]
    groups = lax.axis_size("grp")
    far = lax.axis_size("z")
    near = lax.axis_size("x") * lax.axis_size("c")
    half = columns // 2
    size = iface_sizes
    field, rounded = ((reach, columns), F32), ((reach, columns), BF16)

    heads, = call(heads_kernel, [((reach + 16, columns), jnp.int16)], 2 * reach * width * columns, 2 << 20)(nmat, load)
    heads = passed_along(heads, -1)
    spread, = call(
        functools.partial(tile_kernel, near, far),
        [((near, tile.shape[0] + 16, tile.shape[1] // near), jnp.int16)],
        size=2 << 20,
    )(tile)
    tiles = exchange(spread, ("x", "c"))
    tiles, = call(
        parts_kernel, [((near, 2 * tile.shape[0], tile.shape[1] // near), BF16)], size=2 << 20
    )(tiles)
    turn = call(turn_kernel, [((reach, width), BF16)] * 2, 6 * reach**3, 4 << 20)
    n_own, n_away = turn(nmat)
    n_away = passed_along(n_away, -1)
    d_own, d_away = turn(dmat)
    d_away = pltpu.with_memory_space_constraint(passed_along(d_away, -1), pltpu.VMEM)

    (w_hi, w_lo), (wt_hi, wt_lo) = wave_parts(size[0, 0], directions, reach)

    short = tall = 2 * waves + 8
    flops = 2 * reach * 2 * width * columns

    def pay(rows):
        return ((far, rows, half), F32 if rows == 8 else jnp.int16)

    def solve(payload, extra):
        got = exchange(payload, "z")
        terms, = call(
            functools.partial(coarse_kernel, extra, groups),
            [((groups * near, got.shape[1], half), jnp.int16)],
            6 * near * 4 * waves * far * waves * columns,
            2 << 20,
        )(tiles, got)
        return exchange(terms, SPREAD)

    def halo(rounded_x):
        return passed_along(rounded_x, 1), passed_along(rounded_x, -1)

    def apply(mode, mats, x, xr, rows, *rest):
        before, after = halo(xr)
        inner, = call(inner_kernel, [field], flops // 2, 1 << 20)(*mats, xr)
        smem = pl.BlockSpec(memory_space=pltpu.SMEM)
        vmem = pl.BlockSpec(memory_space=pltpu.VMEM)
        count = 8 + len(rest)
        return pl.pallas_call(
            functools.partial(apply_kernel, mode),
            out_shape=[
                jax.ShapeDtypeStruct(*field),
                jax.ShapeDtypeStruct(*pay(rows)),
            ],
            in_specs=[smem] + [vmem] * count,
            compiler_params=GRANT,
            cost_estimate=pl.CostEstimate(flops=flops, bytes_accessed=4 << 20, transcendentals=0),
        )(size, mats[0], mats[1], inner, x, before, after, wt_hi, wt_lo, *rest)

    rhs, payload = pl.pallas_call(
        rhs_kernel,
        out_shape=[jax.ShapeDtypeStruct(*field), jax.ShapeDtypeStruct(*pay(short))],
        in_specs=[pl.BlockSpec(memory_space=pltpu.SMEM)]
        + [pl.BlockSpec(memory_space=pltpu.VMEM)] * 5,
        name="rhs",
        compiler_params=GRANT,
    )(size, nmat, load, heads, wt_hi, wt_lo)

    n_mats, d_mats = (n_own, n_away), (d_own, d_away)
    dual, dual_r = call(first_kernel, [field, rounded])(solve(payload, False), w_hi, w_lo)
    res, payload = apply("start", n_mats, dual, dual_r, short, rhs)
    rows, x, xr = call(
        project_kernel, [((waves, columns), F32), field, rounded]
    )(solve(payload, False), w_hi, w_lo, res)
    rho = direction = None
    for step in range(ITERS):
        pre, payload = apply("mid", d_mats, x, xr, tall)
        old = () if step == 0 else (rho, direction)
        rho, direction, dir_r = call(
            functools.partial(search_kernel, step == 0), [((8, columns), F32), field, rounded]
        )(solve(payload, True), w_hi, w_lo, pre, *old)
        if step < ITERS - 1:
            image, payload = apply("mid", n_mats, direction, dir_r, tall)
            dual, res, x, xr = call(step_kernel, [field, field, field, rounded])(
                solve(payload, True), w_hi, w_lo, rho, direction, image, dual, res, rows
            )
        else:
            image, payload = apply("last", n_mats, direction, dir_r, 8)
            got = exchange(payload, "z")
            terms, = call(partial_kernel, [((groups * near, 8, half), F32)])(got)
            dual, res = call(final_kernel, [field, field])(
                exchange(terms, SPREAD), rho, direction, image, dual, res
            )
    return dual[None, None], res[None, None]


def solution(mesh):
    finer = Mesh(mesh.devices.reshape(mesh.shape["grp"], 8, 4, 2), ("grp", "z", "x", "c"))
    spec = P("grp", SUB, None, None)

    return jax.shard_map(
        shards,
        mesh=finer,
        in_specs=(spec, spec, spec, spec, P("grp", SUB), P("grp", SUB, None)),
        out_specs=(spec, spec),
        check_vma=False,
    )
```

profile of v0, /device:TPU:1, one launch (start us, length us, event | category | flops | bytes accessed | tf_op | source)
XLA Modules:
  0.0 275.7 jit_solution(5487588658100371022)
XLA Ops:
  0.6 1.6 copy-done.2
  2.2 1.0 copy-done.8
  3.3 1.2 shard_map.81
  4.5 3.2 %collective-permute-start.2 = (s16[528,256]{1,0:T(8,128)(2,1)}, s16[528,256]{1,0:T(8,128)(2,1)}, u32[]{:S(2)}, u32[]{:S(2)}) collective-permute-start(s16[528,256]{1,0:T(8,128)(2,1)} %shard_map.81), channel_id=1, source_target_pairs={{1,0},{2,1},{3,2},{4,3},{5,4},{6,5},{7,6},{8,7},{9,8},{10,9},{11,1... | collective-permute-start | bytes 811016 | tf_op jit(solution)/shard_map/ppermute | solution.py:315
  7.7 1.8 shard_map.78
  9.5 9.2 %all-to-all-start = ((s16[8,144,256]{2,1,0:T(8,128)(2,1)}), s16[8,144,256]{2,1,0:T(8,128)(2,1)S(1)}, u32[]{:S(2)}, u32[]{:S(2)}) async-start(s16[8,144,256]{2,1,0:T(8,128)(2,1)} %shard_map.78), calls=%async_computation | async-start | bytes 1179648 | tf_op jit(solution)/shard_map/all_to_all | solution.py:319
  19.8 2.8 %rhs.1 = (f32[512,256]{1,0:T(8,128)S(1)}, s16[8,72,128]{2,1,0:T(8,128)(2,1)S(1)}) custom-call(s32[1,1]{1,0:T(1,128)} %copy.9.size_ref, bf16[1024,1024]{1,0:T(8,128)(2,1)S(1)} %bitcast.11, bf16[1024,256]{1,0:T(8,128)(2,1)S(1)} %bitcast.14, s16[528,256]{1,0:T(8,128)(2,1)} %collective-permute-done.2.heads_ref, bf16[32,512]{1,0:T(8,128)(2,1)S(1)} %get-tuple-element.71.wt_hi, ...), custom_call_target="tpu_custom_call" | custom-call | tf_op jit(solution)/shard_map/rhs/pallas_call | solution.py:391
  23.4 5.4 %all-to-all-done.got_ref = s16[8,144,256]{2,1,0:T(8,128)(2,1)S(1)} async-done(((s16[8,144,256]{2,1,0:T(8,128)(2,1)}), s16[8,144,256]{2,1,0:T(8,128)(2,1)S(1)}, u32[]{:S(2)}, u32[]{:S(2)}) %all-to-all-start) | async-done | bytes 589856 | tf_op jit(solution)/shard_map/all_to_all | solution.py:319
  28.8 3.4 %all-to-all-start.1 = ((s16[8,72,128]{2,1,0:T(8,128)(2,1)}), s16[8,72,128]{2,1,0:T(8,128)(2,1)S(1)}, u32[]{:S(2)}, u32[]{:S(2)}) async-start(s16[8,72,128]{2,1,0:T(8,128)(2,1)} %copy-done.17), calls=%async_computation.1 | async-start | bytes 294912 | tf_op jit(solution)/shard_map/all_to_all | solution.py:319
  32.2 1.6 copy-done.4
  33.8 2.3 shard_map.77
  36.0 1.0 collective-permute-start
  37.0 1.1 copy-done.6
  38.3 1.7 all-to-all-done.1.got_ref
  41.5 7.8 %all-to-all-start.2 = ((s16[32,72,128]{2,1,0:T(8,128)(2,1)}), s16[32,72,128]{2,1,0:T(8,128)(2,1)}, u32[]{:S(2)}, u32[]{:S(2)}) async-start(s16[32,72,128]{2,1,0:T(8,128)(2,1)} %copy-done.7), calls=%async_computation.2 | async-start | bytes 1179648 | tf_op jit(solution)/shard_map/all_to_all | solution.py:319
  49.2 1.0 fusion
  50.2 11.2 %all-to-all-done.2.got_ref = s16[32,72,128]{2,1,0:T(8,128)(2,1)} async-done(((s16[32,72,128]{2,1,0:T(8,128)(2,1)}), s16[32,72,128]{2,1,0:T(8,128)(2,1)}, u32[]{:S(2)}, u32[]{:S(2)}) %all-to-all-start.2) | async-done | bytes 589856 | tf_op jit(solution)/shard_map/all_to_all | solution.py:319
  61.4 1.6 shard_map.83
  63.6 1.3 collective-permute-start.3
  65.3 3.6 %collective-permute-done.4.next_ref = bf16[512,256]{1,0:T(8,128)(2,1)S(1)} collective-permute-done((bf16[512,256]{1,0:T(8,128)(2,1)S(1)}, bf16[512,256]{1,0:T(8,128)(2,1)S(1)}, u32[]{:S(2)}, u32[]{:S(2)}) %collective-permute-start.4) | collective-permute-done | bytes 262176 | tf_op jit(solution)/shard_map/ppermute | solution.py:315
  71.4 4.2 %all-to-all-start.3 = ((s16[8,72,128]{2,1,0:T(8,128)(2,1)}), s16[8,72,128]{2,1,0:T(8,128)(2,1)}, u32[]{:S(2)}, u32[]{:S(2)}) async-start(s16[8,72,128]{2,1,0:T(8,128)(2,1)} %copy-done.18), calls=%async_computation.3 | async-start | bytes 294912 | tf_op jit(solution)/shard_map/all_to_all | solution.py:319
  75.7 1.6 copy-done.19
  77.3 2.3 shard_map.80
  79.5 1.0 copy-done
  80.5 8.4 %collective-permute-start.1 = (bf16[512,1024]{1,0:T(8,128)(2,1)}, bf16[512,1024]{1,0:T(8,128)(2,1)}, u32[]{:S(2)}, u32[]{:S(2)}) collective-permute-start(bf16[512,1024]{1,0:T(8,128)(2,1)} %get-tuple-element.38), channel_id=1, source_target_pairs={{1,0},{2,1},{3,2},{4,3},{5,4},{6,5},{7,6},{8,7},{9,8},{10,9},{11,1... | collective-permute-start | bytes 3145736 | tf_op jit(solution)/shard_map/ppermute | solution.py:315
  88.9 1.7 shard_map.86
  90.6 19.4 %all_to_all.65.got_ref = s16[32,72,128]{2,1,0:T(8,128)(2,1)S(1)} all-to-all(s16[32,72,128]{2,1,0:T(8,128)(2,1)S(1)} %shard_map.86), channel_id=1, replica_groups=mesh['grp'=4,'z'=8,'x'=4,'c'=2] {'grp','x','c'}, dimensions={0} | all-to-all | bytes 1179648 | tf_op jit(solution)/shard_map/all_to_all | solution.py:319
  111.0 1.3 collective-permute-start.5
  112.3 1.7 shard_map.88.inner_ref
  114.0 2.4 collective-permute-done.6.next_ref
  116.4 2.1 shard_map.89
  118.4 13.7 %all_to_all.66.got_ref = s16[8,72,128]{2,1,0:T(8,128)(2,1)S(1)} all-to-all(s16[8,72,128]{2,1,0:T(8,128)(2,1)S(1)} %get-tuple-element.47), channel_id=1, replica_groups=mesh['grp'=4,'z'=8,'x'=4,'c'=2] {'z'}, dimensions={0} | all-to-all | bytes 294912 | tf_op jit(solution)/shard_map/all_to_all | solution.py:319
  132.9 25.1 %all_to_all.67.got_ref = s16[32,72,128]{2,1,0:T(8,128)(2,1)S(1)} all-to-all(s16[32,72,128]{2,1,0:T(8,128)(2,1)S(1)} %shard_map.90), channel_id=1, replica_groups=mesh['grp'=4,'z'=8,'x'=4,'c'=2] {'grp','x','c'}, dimensions={0} | all-to-all | bytes 1179648 | tf_op jit(solution)/shard_map/all_to_all | solution.py:319
  159.0 1.3 collective-permute-start.7
  160.8 3.6 %collective-permute-done.8.next_ref = bf16[512,256]{1,0:T(8,128)(2,1)S(1)} collective-permute-done((bf16[512,256]{1,0:T(8,128)(2,1)S(1)}, bf16[512,256]{1,0:T(8,128)(2,1)S(1)}, u32[]{:S(2)}, u32[]{:S(2)}) %collective-permute-start.8) | collective-permute-done | bytes 262176 | tf_op jit(solution)/shard_map/ppermute | solution.py:315
  165.3 10.6 %all_to_all.68.got_ref = s16[8,72,128]{2,1,0:T(8,128)(2,1)S(1)} all-to-all(s16[8,72,128]{2,1,0:T(8,128)(2,1)S(1)} %get-tuple-element.51), channel_id=1, replica_groups=mesh['grp'=4,'z'=8,'x'=4,'c'=2] {'z'}, dimensions={0} | all-to-all | bytes 294912 | tf_op jit(solution)/shard_map/all_to_all | solution.py:319
  176.6 22.2 %all_to_all.69.got_ref = s16[32,72,128]{2,1,0:T(8,128)(2,1)S(1)} all-to-all(s16[32,72,128]{2,1,0:T(8,128)(2,1)S(1)} %shard_map.94), channel_id=1, replica_groups=mesh['grp'=4,'z'=8,'x'=4,'c'=2] {'grp','x','c'}, dimensions={0} | all-to-all | bytes 1179648 | tf_op jit(solution)/shard_map/all_to_all | solution.py:319
  200.0 1.3 collective-permute-start.9
  201.3 1.7 shard_map.96.inner_ref
  203.0 2.4 collective-permute-done.10.next_ref
  205.3 2.0 shard_map.97
  207.4 10.5 %all_to_all.70.got_ref = s16[8,72,128]{2,1,0:T(8,128)(2,1)S(1)} all-to-all(s16[8,72,128]{2,1,0:T(8,128)(2,1)S(1)} %get-tuple-element.57), channel_id=1, replica_groups=mesh['grp'=4,'z'=8,'x'=4,'c'=2] {'z'}, dimensions={0} | all-to-all | bytes 294912 | tf_op jit(solution)/shard_map/all_to_all | solution.py:319
  218.6 22.2 %all_to_all.71.got_ref = s16[32,72,128]{2,1,0:T(8,128)(2,1)S(1)} all-to-all(s16[32,72,128]{2,1,0:T(8,128)(2,1)S(1)} %shard_map.98), channel_id=1, replica_groups=mesh['grp'=4,'z'=8,'x'=4,'c'=2] {'grp','x','c'}, dimensions={0} | all-to-all | bytes 1179648 | tf_op jit(solution)/shard_map/all_to_all | solution.py:319
  241.8 1.3 collective-permute-start.11
  243.6 3.6 %collective-permute-done.12.next_ref = bf16[512,256]{1,0:T(8,128)(2,1)S(1)} collective-permute-done((bf16[512,256]{1,0:T(8,128)(2,1)S(1)}, bf16[512,256]{1,0:T(8,128)(2,1)S(1)}, u32[]{:S(2)}, u32[]{:S(2)}) %collective-permute-start.12) | collective-permute-done | bytes 262176 | tf_op jit(solution)/shard_map/ppermute | solution.py:315
  247.7 9.2 %all_to_all.72.got_ref = f32[8,8,128]{2,1,0:T(8,128)S(1)} all-to-all(f32[8,8,128]{2,1,0:T(8,128)S(1)} %get-tuple-element.61), channel_id=1, replica_groups=mesh['grp'=4,'z'=8,'x'=4,'c'=2] {'z'}, dimensions={0} | all-to-all | bytes 65536 | tf_op jit(solution)/shard_map/all_to_all | solution.py:319
  256.9 17.7 %all_to_all.73.got_ref = f32[32,8,128]{2,1,0:T(8,128)S(1)} all-to-all(f32[32,8,128]{2,1,0:T(8,128)S(1)} %shard_map.102), channel_id=1, replica_groups=mesh['grp'=4,'z'=8,'x'=4,'c'=2] {'grp','x','c'}, dimensions={0} | all-to-all | bytes 262144 | tf_op jit(solution)/shard_map/all_to_all | solution.py:319
  274.6 1.1 shard_map.103
  (71 shorter events, 14.7 us)
Async XLA Ops:
  0.6 1.6 copy-start.2
  2.2 1.0 copy-start.8
  3.3 4.4 %copy-start.14 = (f32[1,1,128,2048]{3,2,1,0:T(8,128)S(1)}, f32[1,1,128,2048]{3,2,1,0:T(8,128)}, u32[]{:S(2)}) copy-start(f32[1,1,128,2048]{3,2,1,0:T(8,128)} %param.8) | copy-start | bytes 3145732
  4.5 14.9 %copy-start.20 = (s32[1,1,32]{2,1,0:T(1,128)S(1)}, s32[1,1,32]{2,1,0:T(1,128)}, u32[]{:S(2)}) copy-start(s32[1,1,32]{2,1,0:T(1,128)} %param.11) | copy-start | bytes 388
  4.5 15.3 %copy-start.3 = (bf16[1,1,1024,1024]{3,2,1,0:T(8,128)(2,1)S(1)}, bf16[1,1,1024,1024]{3,2,1,0:T(8,128)(2,1)}, u32[]{:S(2)}) copy-start(bf16[1,1,1024,1024]{3,2,1,0:T(8,128)(2,1)} %param.6) | copy-start | bytes 6291460
  4.5 15.3 %copy-start.9 = (bf16[1,1,1024,256]{3,2,1,0:T(8,128)(2,1)S(1)}, bf16[1,1,1024,256]{3,2,1,0:T(8,128)(2,1)}, u32[]{:S(2)}) copy-start(bf16[1,1,1024,256]{3,2,1,0:T(8,128)(2,1)} %param.9) | copy-start | bytes 1572868
  4.5 15.2 %collective-permute-start.2 = (s16[528,256]{1,0:T(8,128)(2,1)}, s16[528,256]{1,0:T(8,128)(2,1)}, u32[]{:S(2)}, u32[]{:S(2)}) collective-permute-start(s16[528,256]{1,0:T(8,128)(2,1)} %shard_map.81), channel_id=1, source_target_pairs={{1,0},{2,1},{3,2},{4,3},{5,4},{6,5},{7,6},{8,7},{9,8},{10,9},{11,1... | collective-permute-start | bytes 811016 | tf_op jit(solution)/shard_map/ppermute | solution.py:315
  9.5 19.3 %all-to-all-start = ((s16[8,144,256]{2,1,0:T(8,128)(2,1)}), s16[8,144,256]{2,1,0:T(8,128)(2,1)S(1)}, u32[]{:S(2)}, u32[]{:S(2)}) async-start(s16[8,144,256]{2,1,0:T(8,128)(2,1)} %shard_map.78), calls=%async_computation | async-start | bytes 1179648 | tf_op jit(solution)/shard_map/all_to_all | solution.py:319
  22.6 0.8 copy-start.15
  23.4 5.4 %copy-start.17 = (s16[8,72,128]{2,1,0:T(8,128)(2,1)}, s16[8,72,128]{2,1,0:T(8,128)(2,1)S(1)}, u32[]{:S(2)}) copy-start(s16[8,72,128]{2,1,0:T(8,128)(2,1)S(1)} %get-tuple-element.39) | copy-start | bytes 442372
  28.8 7.3 %copy-start.5 = (s16[8,144,256]{2,1,0:T(8,128)(2,1)}, s16[8,144,256]{2,1,0:T(8,128)(2,1)S(1)}, u32[]{:S(2)}) copy-start(s16[8,144,256]{2,1,0:T(8,128)(2,1)S(1)} %all-to-all-done.got_ref) | copy-start | bytes 1769476
  28.8 11.2 %all-to-all-start.1 = ((s16[8,72,128]{2,1,0:T(8,128)(2,1)}), s16[8,72,128]{2,1,0:T(8,128)(2,1)S(1)}, u32[]{:S(2)}, u32[]{:S(2)}) async-start(s16[8,72,128]{2,1,0:T(8,128)(2,1)} %copy-done.17), calls=%async_computation.1 | async-start | bytes 294912 | tf_op jit(solution)/shard_map/all_to_all | solution.py:319
  32.2 1.6 copy-start.4
  36.0 28.9 %collective-permute-start = (bf16[512,1024]{1,0:T(8,128)(2,1)}, bf16[512,1024]{1,0:T(8,128)(2,1)S(1)}, u32[]{:S(2)}, u32[]{:S(2)}) collective-permute-start(bf16[512,1024]{1,0:T(8,128)(2,1)} %get-tuple-element.36), channel_id=1, source_target_pairs={{1,0},{2,1},{3,2},{4,3},{5,4},{6,5},{7,6},{8,7},{9,8},{10,9},{11,1... | collective-permute-start | bytes 3145736 | tf_op jit(solution)/shard_map/ppermute | solution.py:315
  37.0 1.1 copy-start.6
  40.7 0.8 copy-start.7
  41.5 19.9 %all-to-all-start.2 = ((s16[32,72,128]{2,1,0:T(8,128)(2,1)}), s16[32,72,128]{2,1,0:T(8,128)(2,1)}, u32[]{:S(2)}, u32[]{:S(2)}) async-start(s16[32,72,128]{2,1,0:T(8,128)(2,1)} %copy-done.7), calls=%async_computation.2 | async-start | bytes 1179648 | tf_op jit(solution)/shard_map/all_to_all | solution.py:319
  61.4 7.7 %copy-start.16 = (f32[512,256]{1,0:T(8,128)S(1)}, f32[512,256]{1,0:T(8,128)}, u32[]{:S(2)}) copy-start(f32[512,256]{1,0:T(8,128)} %copy-done.15) | copy-start | bytes 1572868
  63.1 6.9 %copy-start.10 = (f32[512,256]{1,0:T(8,128)}, f32[512,256]{1,0:T(8,128)S(1)}, u32[]{:S(2)}) copy-start(f32[512,256]{1,0:T(8,128)S(1)} %get-tuple-element.41.x_ref.dual_ref) | copy-start | bytes 1572868
  63.1 5.9 %collective-permute-start.4 = (bf16[512,256]{1,0:T(8,128)(2,1)S(1)}, bf16[512,256]{1,0:T(8,128)(2,1)S(1)}, u32[]{:S(2)}, u32[]{:S(2)}) collective-permute-start(bf16[512,256]{1,0:T(8,128)(2,1)S(1)} %get-tuple-element.40.xr_ref), channel_id=1, source_target_pairs={{1,0},{2,1},{3,2},{4,3},{5,4},{6,5},{7,6},{8,7},{9,8},{10,9},{11,1... | collective-permute-start | bytes 786440 | tf_op jit(solution)/shard_map/ppermute | solution.py:315
  63.6 5.6 %collective-permute-start.3 = (bf16[512,256]{1,0:T(8,128)(2,1)S(1)}, bf16[512,256]{1,0:T(8,128)(2,1)S(1)}, u32[]{:S(2)}, u32[]{:S(2)}) collective-permute-start(bf16[512,256]{1,0:T(8,128)(2,1)S(1)} %get-tuple-element.40.xr_ref), channel_id=1, source_target_pairs={{63,0},{0,1},{1,2},{2,3},{3,4},{4,5},{5,6},{6,7},{7,8},{8,9},{9,10... | collective-permute-start | bytes 786440 | tf_op jit(solution)/shard_map/ppermute | solution.py:315
  70.0 0.8 copy-start.12
  70.8 0.7 copy-start.18
  71.4 17.4 %all-to-all-start.3 = ((s16[8,72,128]{2,1,0:T(8,128)(2,1)}), s16[8,72,128]{2,1,0:T(8,128)(2,1)}, u32[]{:S(2)}, u32[]{:S(2)}) async-start(s16[8,72,128]{2,1,0:T(8,128)(2,1)} %copy-done.18), calls=%async_computation.3 | async-start | bytes 294912 | tf_op jit(solution)/shard_map/all_to_all | solution.py:319
  75.7 1.6 copy-start.19
  79.5 1.0 copy-start
  80.5 31.8 %collective-permute-start.1 = (bf16[512,1024]{1,0:T(8,128)(2,1)}, bf16[512,1024]{1,0:T(8,128)(2,1)}, u32[]{:S(2)}, u32[]{:S(2)}) collective-permute-start(bf16[512,1024]{1,0:T(8,128)(2,1)} %get-tuple-element.38), channel_id=1, source_target_pairs={{1,0},{2,1},{3,2},{4,3},{5,4},{6,5},{7,6},{8,7},{9,8},{10,9},{11,1... | collective-permute-start | bytes 3145736 | tf_op jit(solution)/shard_map/ppermute | solution.py:315
  88.9 21.1 %copy-start.13 = (f32[512,256]{1,0:T(8,128)S(1)}, f32[512,256]{1,0:T(8,128)}, u32[]{:S(2)}) copy-start(f32[512,256]{1,0:T(8,128)} %copy-done.12) | copy-start | bytes 1572868
  88.9 23.4 %copy-start.1 = (bf16[512,1024]{1,0:T(8,128)(2,1)S(1)}, bf16[512,1024]{1,0:T(8,128)(2,1)}, u32[]{:S(2)}) copy-start(bf16[512,1024]{1,0:T(8,128)(2,1)} %copy-done) | copy-start | bytes 3145732
  110.5 5.9 %collective-permute-start.6 = (bf16[512,256]{1,0:T(8,128)(2,1)S(1)}, bf16[512,256]{1,0:T(8,128)(2,1)S(1)}, u32[]{:S(2)}, u32[]{:S(2)}) collective-permute-start(bf16[512,256]{1,0:T(8,128)(2,1)S(1)} %get-tuple-element.45.xr_ref), channel_id=1, source_target_pairs={{1,0},{2,1},{3,2},{4,3},{5,4},{6,5},{7,6},{8,7},{9,8},{10,9},{11,1... | collective-permute-start | bytes 786440 | tf_op jit(solution)/shard_map/ppermute | solution.py:315
  111.0 5.4 %collective-permute-start.5 = (bf16[512,256]{1,0:T(8,128)(2,1)S(1)}, bf16[512,256]{1,0:T(8,128)(2,1)S(1)}, u32[]{:S(2)}, u32[]{:S(2)}) collective-permute-start(bf16[512,256]{1,0:T(8,128)(2,1)S(1)} %get-tuple-element.45.xr_ref), channel_id=1, source_target_pairs={{63,0},{0,1},{1,2},{2,3},{3,4},{4,5},{5,6},{6,7},{7,8},{8,9},{9,10... | collective-permute-start | bytes 786440 | tf_op jit(solution)/shard_map/ppermute | solution.py:315
  158.5 5.9 %collective-permute-start.8 = (bf16[512,256]{1,0:T(8,128)(2,1)S(1)}, bf16[512,256]{1,0:T(8,128)(2,1)S(1)}, u32[]{:S(2)}, u32[]{:S(2)}) collective-permute-start(bf16[512,256]{1,0:T(8,128)(2,1)S(1)} %get-tuple-element.49.xr_ref), channel_id=1, source_target_pairs={{1,0},{2,1},{3,2},{4,3},{5,4},{6,5},{7,6},{8,7},{9,8},{10,9},{11,1... | collective-permute-start | bytes 786440 | tf_op jit(solution)/shard_map/ppermute | solution.py:315
  159.0 5.4 %collective-permute-start.7 = (bf16[512,256]{1,0:T(8,128)(2,1)S(1)}, bf16[512,256]{1,0:T(8,128)(2,1)S(1)}, u32[]{:S(2)}, u32[]{:S(2)}) collective-permute-start(bf16[512,256]{1,0:T(8,128)(2,1)S(1)} %get-tuple-element.49.xr_ref), channel_id=1, source_target_pairs={{63,0},{0,1},{1,2},{2,3},{3,4},{4,5},{5,6},{6,7},{7,8},{8,9},{9,10... | collective-permute-start | bytes 786440 | tf_op jit(solution)/shard_map/ppermute | solution.py:315
  165.2 33.6 %copy-start.11 = (f32[512,256]{1,0:T(8,128)S(1)}, f32[512,256]{1,0:T(8,128)}, u32[]{:S(2)}) copy-start(f32[512,256]{1,0:T(8,128)} %copy-done.10) | copy-start | bytes 1572868
  199.5 5.9 %collective-permute-start.10 = (bf16[512,256]{1,0:T(8,128)(2,1)S(1)}, bf16[512,256]{1,0:T(8,128)(2,1)S(1)}, u32[]{:S(2)}, u32[]{:S(2)}) collective-permute-start(bf16[512,256]{1,0:T(8,128)(2,1)S(1)} %get-tuple-element.55.xr_ref), channel_id=1, source_target_pairs={{1,0},{2,1},{3,2},{4,3},{5,4},{6,5},{7,6},{8,7},{9,8},{10,9},{11,1... | collective-permute-start | bytes 786440 | tf_op jit(solution)/shard_map/ppermute | solution.py:315
  200.0 5.4 %collective-permute-start.9 = (bf16[512,256]{1,0:T(8,128)(2,1)S(1)}, bf16[512,256]{1,0:T(8,128)(2,1)S(1)}, u32[]{:S(2)}, u32[]{:S(2)}) collective-permute-start(bf16[512,256]{1,0:T(8,128)(2,1)S(1)} %get-tuple-element.55.xr_ref), channel_id=1, source_target_pairs={{63,0},{0,1},{1,2},{2,3},{3,4},{4,5},{5,6},{6,7},{7,8},{8,9},{9,10... | collective-permute-start | bytes 786440 | tf_op jit(solution)/shard_map/ppermute | solution.py:315
  241.3 5.9 %collective-permute-start.12 = (bf16[512,256]{1,0:T(8,128)(2,1)S(1)}, bf16[512,256]{1,0:T(8,128)(2,1)S(1)}, u32[]{:S(2)}, u32[]{:S(2)}) collective-permute-start(bf16[512,256]{1,0:T(8,128)(2,1)S(1)} %get-tuple-element.59.xr_ref), channel_id=1, source_target_pairs={{1,0},{2,1},{3,2},{4,3},{5,4},{6,5},{7,6},{8,7},{9,8},{10,9},{11,1... | collective-permute-start | bytes 786440 | tf_op jit(solution)/shard_map/ppermute | solution.py:315
  241.8 5.4 %collective-permute-start.11 = (bf16[512,256]{1,0:T(8,128)(2,1)S(1)}, bf16[512,256]{1,0:T(8,128)(2,1)S(1)}, u32[]{:S(2)}, u32[]{:S(2)}) collective-permute-start(bf16[512,256]{1,0:T(8,128)(2,1)S(1)} %get-tuple-element.59.xr_ref), channel_id=1, source_target_pairs={{63,0},{0,1},{1,2},{2,3},{3,4},{4,5},{5,6},{6,7},{7,8},{8,9},{9,10... | collective-permute-start | bytes 786440 | tf_op jit(solution)/shard_map/ppermute | solution.py:315
where the time goes:
time: 277 us; the launch traced here: 276 us
  blocking collectives  151 us (55%)
  starting transfers between devices  46.2 us (17%)
  waiting for transfers between devices  34.1 us (12%)
  Pallas kernels  30.7 us (11%)
  local copies, waits for them, and re-layouts  10.9 us (4%)
    all_to_all x9, blocking collectives, exchange(): return lax.all_to_all(value, axes, 0, 0, tiled=True)  151 us
    all_to_all x4, starting transfers between devices, exchange(): return lax.all_to_all(value, axes, 0, 0, tiled=True)  24.6 us
    ppermute x13, starting transfers between devices, passed_along(): return lax.ppermute(block, SUB, [((i - distance) % n, i) for i in range(n)])  21.7 us
    all_to_all x4, waiting for transfers between devices, exchange(): return lax.all_to_all(value, axes, 0, 0, tiled=True)  18.3 us
    ppermute x13, waiting for transfers between devices, passed_along(): return lax.ppermute(block, SUB, [((i - distance) % n, i) for i in range(n)])  15.8 us
    unnamed x42, local copies, waits for them, and re-layouts  10.9 us
    pallas_call x5, Pallas kernels, apply(): pl.pallas_call(functools.partial(apply_kernel, mode), out_shape=[jax.Shap...  6.19 us
  transfers between devices with their start and end apart: 17, of which 9 were waited for; matrix products, arithmetic and copies ran while one was open for 0% of the time, Pallas kernels for 7%

commit v1 on v0

--- a/solution.py
+++ b/solution.py
@@ -12,7 +12,8 @@
 ITERS = 2
 WAVE_NUMBER = 0.785
 SUB = ("z", "x", "c")
-SPREAD = ("grp", "x", "c")
+GATHER = ("z", "c")
+SPREAD = ("grp", "x")
 F32 = jnp.float32
 BF16 = jnp.bfloat16
 GRANT = pltpu.CompilerParams(vmem_limit_bytes=14 << 20)
@@ -327,8 +328,8 @@
     directions = wave_dirs[0, 0]
     waves = directions.shape[0]
     groups = lax.axis_size("grp")
-    far = lax.axis_size("z")
-    near = lax.axis_size("x") * lax.axis_size("c")
+    near = lax.axis_size("x")
+    far = lax.axis_size(GATHER)
     half = columns // 2
     size = iface_sizes
     field, rounded = ((reach, columns), F32), ((reach, columns), BF16)
@@ -336,11 +337,11 @@
     heads, = call(heads_kernel, [((reach + 16, columns), jnp.int16)], 2 * reach * width * columns, 2 << 20)(nmat, load)
     heads = passed_along(heads, -1)
     spread, = call(
-        functools.partial(tile_kernel, near, far),
+        functools.partial(tile_kernel, near, lax.axis_size("z")),
         [((near, tile.shape[0] + 16, tile.shape[1] // near), jnp.int16)],
         size=2 << 20,
     )(tile)
-    tiles = exchange(spread, ("x", "c"))
+    tiles = exchange(spread, "x")
     tiles, = call(
         parts_kernel, [((near, 2 * tile.shape[0], tile.shape[1] // near), BF16)], size=2 << 20
     )(tiles)
@@ -359,7 +360,7 @@
         return ((far, rows, half), F32 if rows == 8 else jnp.int16)
 
     def solve(payload, extra):
-        got = exchange(payload, "z")
+        got = exchange(payload, GATHER)
         terms, = call(
             functools.partial(coarse_kernel, extra, groups),
             [((groups * near, got.shape[1], half), jnp.int16)],
@@ -417,7 +418,7 @@
             )
         else:
             image, payload = apply("last", n_mats, direction, dir_r, 8)
-            got = exchange(payload, "z")
+            got = exchange(payload, GATHER)
             terms, = call(partial_kernel, [((groups * near, 8, half), F32)])(got)
             dual, res = call(final_kernel, [field, field])(
                 exchange(terms, SPREAD), rho, direction, image, dual, res

time: 277 us -> 265 us (0.957)
  blocking collectives: 151 us -> 135 us
  waiting for transfers between devices: 34.1 us -> 40 us
  starting transfers between devices: 46.2 us -> 43.2 us
    all_to_all x9, blocking collectives: 151 us -> 135 us  [exchange(): return lax.all_to_all(value, axes, 0, 0, tiled=True)]
    ppermute x13, starting transfers between devices: 21.7 us -> 12.6 us  [passed_along(): return lax.ppermute(block, SUB, [((i - distance) % n, i) for i in range(n)])]
    all_to_all x4, waiting for transfers between devices: 18.3 us -> 24.4 us  [exchange(): return lax.all_to_all(value, axes, 0, 0, tiled=True)]
    all_to_all x4, starting transfers between devices: 24.6 us -> 30.6 us  [exchange(): return lax.all_to_all(value, axes, 0, 0, tiled=True)]
  transfers between devices with their start and end apart: 17 -> 17, of which waited for: 9 -> 9; matrix products, arithmetic and copies ran while one was open for 0% -> 1% of each run, Pallas kernels for 7% -> 7%
where the time goes in v1:
time: 265 us; the launch traced here: 264 us
  blocking collectives  135 us (51%)
  starting transfers between devices  43.2 us (16%)
  waiting for transfers between devices  40 us (15%)
  Pallas kernels  30.8 us (12%)
  local copies, waits for them, and re-layouts  11.6 us (4%)
    all_to_all x9, blocking collectives, exchange(): return lax.all_to_all(value, axes, 0, 0, tiled=True)  135 us
    all_to_all x4, starting transfers between devices, exchange(): return lax.all_to_all(value, axes, 0, 0, tiled=True)  30.6 us
    all_to_all x4, waiting for transfers between devices, exchange(): return lax.all_to_all(value, axes, 0, 0, tiled=True)  24.4 us
    ppermute x13, waiting for transfers between devices, passed_along(): return lax.ppermute(block, SUB, [((i - distance) % n, i) for i in range(n)])  15.6 us
    ppermute x13, starting transfers between devices, passed_along(): return lax.ppermute(block, SUB, [((i - distance) % n, i) for i in range(n)])  12.6 us
    unnamed x42, local copies, waits for them, and re-layouts  11.6 us
    pallas_call x5, Pallas kernels, apply(): pl.pallas_call(functools.partial(apply_kernel, mode), out_shape=[jax.Shap...  6.24 us
    pallas_call x5, Pallas kernels, solve(): call(functools.partial(coarse_kernel, extra, groups), [((groups * near, g...  5.51 us
  transfers between devices with their start and end apart: 17, of which 9 were waited for; matrix products, arithmetic and copies ran while one was open for 1% of the time, Pallas kernels for 7%

profile of v1, /device:TPU:1, one launch (start us, length us, event | category | flops | bytes accessed | tf_op | source)
XLA Modules:
  0.0 264.0 jit_solution(16237368768408941370)
XLA Ops:
  0.6 1.6 copy-done.2
  2.2 1.0 copy-done.7
  3.3 1.2 shard_map.81
  4.5 3.2 %collective-permute-start.2 = (s16[528,256]{1,0:T(8,128)(2,1)}, s16[528,256]{1,0:T(8,128)(2,1)}, u32[]{:S(2)}, u32[]{:S(2)}) collective-permute-start(s16[528,256]{1,0:T(8,128)(2,1)} %shard_map.81), channel_id=1, source_target_pairs={{1,0},{2,1},{3,2},{4,3},{5,4},{6,5},{7,6},{8,7},{9,8},{10,9},{11,1... | collective-permute-start | bytes 811016 | tf_op jit(solution)/shard_map/ppermute | solution.py:316
  7.7 1.2 shard_map.78
  8.9 3.5 %all-to-all-start = ((s16[4,144,512]{2,1,0:T(8,128)(2,1)}), s16[4,144,512]{2,1,0:T(8,128)(2,1)S(1)}, u32[]{:S(2)}, u32[]{:S(2)}) async-start(s16[4,144,512]{2,1,0:T(8,128)(2,1)} %shard_map.78), calls=%async_computation | async-start | bytes 1179648 | tf_op jit(solution)/shard_map/all_to_all | solution.py:320
  13.5 2.8 %rhs.1 = (f32[512,256]{1,0:T(8,128)S(1)}, s16[16,72,128]{2,1,0:T(8,128)(2,1)S(1)}) custom-call(s32[1,1]{1,0:T(1,128)} %copy.9.size_ref, bf16[1024,1024]{1,0:T(8,128)(2,1)S(1)} %bitcast.11, bf16[1024,256]{1,0:T(8,128)(2,1)S(1)} %bitcast.14, s16[528,256]{1,0:T(8,128)(2,1)} %collective-permute-done.2.heads_ref, bf16[32,512]{1,0:T(8,128)(2,1)S(1)} %get-tuple-element.71.wt_hi, ...), custom_call_target="tpu_custom_call" | custom-call | tf_op jit(solution)/shard_map/rhs/pallas_call | solution.py:392
  17.8 1.9 all-to-all-done.got_ref
  19.7 11.2 %all-to-all-start.1 = ((s16[16,72,128]{2,1,0:T(8,128)(2,1)}), s16[16,72,128]{2,1,0:T(8,128)(2,1)}, u32[]{:S(2)}, u32[]{:S(2)}) async-start(s16[16,72,128]{2,1,0:T(8,128)(2,1)} %copy-done.17), calls=%async_computation.1 | async-start | bytes 589824 | tf_op jit(solution)/shard_map/all_to_all | solution.py:320
  30.9 1.6 copy-done.4
  32.4 2.3 shard_map.77
  34.9 1.1 copy-done.6
  36.2 7.1 %all-to-all-done.1.got_ref = s16[16,72,128]{2,1,0:T(8,128)(2,1)} async-done(((s16[16,72,128]{2,1,0:T(8,128)(2,1)}), s16[16,72,128]{2,1,0:T(8,128)(2,1)}, u32[]{:S(2)}, u32[]{:S(2)}) %all-to-all-start.1) | async-done | bytes 294944 | tf_op jit(solution)/shard_map/all_to_all | solution.py:320
  43.2 1.6 shard_map.82
  45.6 4.9 %all-to-all-start.2 = ((s16[16,72,128]{2,1,0:T(8,128)(2,1)}), s16[16,72,128]{2,1,0:T(8,128)(2,1)}, u32[]{:S(2)}, u32[]{:S(2)}) async-start(s16[16,72,128]{2,1,0:T(8,128)(2,1)} %copy-done.13), calls=%async_computation.2 | async-start | bytes 589824 | tf_op jit(solution)/shard_map/all_to_all | solution.py:320
  50.6 1.0 fusion
  51.6 8.0 %all-to-all-done.2.got_ref = s16[16,72,128]{2,1,0:T(8,128)(2,1)} async-done(((s16[16,72,128]{2,1,0:T(8,128)(2,1)}), s16[16,72,128]{2,1,0:T(8,128)(2,1)}, u32[]{:S(2)}, u32[]{:S(2)}) %all-to-all-start.2) | async-done | bytes 294944 | tf_op jit(solution)/shard_map/all_to_all | solution.py:320
  59.6 1.4 shard_map.83
  61.0 1.1 collective-permute-start.4
  63.3 3.6 %collective-permute-done.4.next_ref = bf16[512,256]{1,0:T(8,128)(2,1)S(1)} collective-permute-done((bf16[512,256]{1,0:T(8,128)(2,1)S(1)}, bf16[512,256]{1,0:T(8,128)(2,1)S(1)}, u32[]{:S(2)}, u32[]{:S(2)}) %collective-permute-start.4) | collective-permute-done | bytes 262176 | tf_op jit(solution)/shard_map/ppermute | solution.py:316
  69.3 11.0 %all-to-all-start.3 = ((s16[16,72,128]{2,1,0:T(8,128)(2,1)}), s16[16,72,128]{2,1,0:T(8,128)(2,1)}, u32[]{:S(2)}, u32[]{:S(2)}) async-start(s16[16,72,128]{2,1,0:T(8,128)(2,1)} %copy-done.18), calls=%async_computation.3 | async-start | bytes 589824 | tf_op jit(solution)/shard_map/all_to_all | solution.py:320
  80.3 1.6 copy-done.19
  81.9 2.3 shard_map.80
  84.2 1.0 copy-done
  85.3 7.4 %all-to-all-done.3.got_ref = s16[16,72,128]{2,1,0:T(8,128)(2,1)} async-done(((s16[16,72,128]{2,1,0:T(8,128)(2,1)}), s16[16,72,128]{2,1,0:T(8,128)(2,1)}, u32[]{:S(2)}, u32[]{:S(2)}) %all-to-all-start.3) | async-done | bytes 294944 | tf_op jit(solution)/shard_map/all_to_all | solution.py:320
  92.7 1.8 shard_map.86
  94.4 11.6 %all_to_all.65.got_ref = s16[16,72,128]{2,1,0:T(8,128)(2,1)S(1)} all-to-all(s16[16,72,128]{2,1,0:T(8,128)(2,1)S(1)} %shard_map.86), channel_id=1, replica_groups=mesh['grp'=4,'z'=8,'x'=4,'c'=2] {'grp','x'}, dimensions={0} | all-to-all | bytes 589824 | tf_op jit(solution)/shard_map/all_to_all | solution.py:320
  106.5 1.1 collective-permute-start.6
  108.3 1.7 shard_map.88.inner_ref
  110.0 2.4 collective-permute-done.6.next_ref
  112.4 2.1 shard_map.89
  114.4 24.4 %all_to_all.66.got_ref = s16[16,72,128]{2,1,0:T(8,128)(2,1)S(1)} all-to-all(s16[16,72,128]{2,1,0:T(8,128)(2,1)S(1)} %get-tuple-element.47), channel_id=1, replica_groups=mesh['grp'=4,'z'=8,'x'=4,'c'=2] {'z','c'}, dimensions={0} | all-to-all | bytes 589824 | tf_op jit(solution)/shard_map/all_to_all | solution.py:320
  139.6 11.9 %all_to_all.67.got_ref = s16[16,72,128]{2,1,0:T(8,128)(2,1)S(1)} all-to-all(s16[16,72,128]{2,1,0:T(8,128)(2,1)S(1)} %shard_map.90), channel_id=1, replica_groups=mesh['grp'=4,'z'=8,'x'=4,'c'=2] {'grp','x'}, dimensions={0} | all-to-all | bytes 589824 | tf_op jit(solution)/shard_map/all_to_all | solution.py:320
  151.9 1.1 collective-permute-start.8
  154.1 3.6 %collective-permute-done.8.next_ref = bf16[512,256]{1,0:T(8,128)(2,1)S(1)} collective-permute-done((bf16[512,256]{1,0:T(8,128)(2,1)S(1)}, bf16[512,256]{1,0:T(8,128)(2,1)S(1)}, u32[]{:S(2)}, u32[]{:S(2)}) %collective-permute-start.8) | collective-permute-done | bytes 262176 | tf_op jit(solution)/shard_map/ppermute | solution.py:316
  158.6 19.8 %all_to_all.68.got_ref = s16[16,72,128]{2,1,0:T(8,128)(2,1)S(1)} all-to-all(s16[16,72,128]{2,1,0:T(8,128)(2,1)S(1)} %get-tuple-element.51), channel_id=1, replica_groups=mesh['grp'=4,'z'=8,'x'=4,'c'=2] {'z','c'}, dimensions={0} | all-to-all | bytes 589824 | tf_op jit(solution)/shard_map/all_to_all | solution.py:320
  179.1 11.8 %all_to_all.69.got_ref = s16[16,72,128]{2,1,0:T(8,128)(2,1)S(1)} all-to-all(s16[16,72,128]{2,1,0:T(8,128)(2,1)S(1)} %shard_map.94), channel_id=1, replica_groups=mesh['grp'=4,'z'=8,'x'=4,'c'=2] {'grp','x'}, dimensions={0} | all-to-all | bytes 589824 | tf_op jit(solution)/shard_map/all_to_all | solution.py:320
  191.5 1.1 collective-permute-start.10
  193.3 1.7 shard_map.96.inner_ref
  194.9 2.4 collective-permute-done.10.next_ref
  197.3 2.1 shard_map.97
  199.4 19.7 %all_to_all.70.got_ref = s16[16,72,128]{2,1,0:T(8,128)(2,1)S(1)} all-to-all(s16[16,72,128]{2,1,0:T(8,128)(2,1)S(1)} %get-tuple-element.57), channel_id=1, replica_groups=mesh['grp'=4,'z'=8,'x'=4,'c'=2] {'z','c'}, dimensions={0} | all-to-all | bytes 589824 | tf_op jit(solution)/shard_map/all_to_all | solution.py:320
  219.8 11.8 %all_to_all.71.got_ref = s16[16,72,128]{2,1,0:T(8,128)(2,1)S(1)} all-to-all(s16[16,72,128]{2,1,0:T(8,128)(2,1)S(1)} %shard_map.98), channel_id=1, replica_groups=mesh['grp'=4,'z'=8,'x'=4,'c'=2] {'grp','x'}, dimensions={0} | all-to-all | bytes 589824 | tf_op jit(solution)/shard_map/all_to_all | solution.py:320
  232.0 1.1 collective-permute-start.12
  234.3 3.6 %collective-permute-done.12.next_ref = bf16[512,256]{1,0:T(8,128)(2,1)S(1)} collective-permute-done((bf16[512,256]{1,0:T(8,128)(2,1)S(1)}, bf16[512,256]{1,0:T(8,128)(2,1)S(1)}, u32[]{:S(2)}, u32[]{:S(2)}) %collective-permute-start.12) | collective-permute-done | bytes 262176 | tf_op jit(solution)/shard_map/ppermute | solution.py:316
  238.4 15.2 %all_to_all.72.got_ref = f32[16,8,128]{2,1,0:T(8,128)S(1)} all-to-all(f32[16,8,128]{2,1,0:T(8,128)S(1)} %get-tuple-element.61), channel_id=1, replica_groups=mesh['grp'=4,'z'=8,'x'=4,'c'=2] {'z','c'}, dimensions={0} | all-to-all | bytes 131072 | tf_op jit(solution)/shard_map/all_to_all | solution.py:320
  253.6 9.3 %all_to_all.73.got_ref = f32[16,8,128]{2,1,0:T(8,128)S(1)} all-to-all(f32[16,8,128]{2,1,0:T(8,128)S(1)} %shard_map.102), channel_id=1, replica_groups=mesh['grp'=4,'z'=8,'x'=4,'c'=2] {'grp','x'}, dimensions={0} | all-to-all | bytes 131072 | tf_op jit(solution)/shard_map/all_to_all | solution.py:320
  262.9 1.1 shard_map.103
  (71 shorter events, 15.8 us)
Async XLA Ops:
  0.6 1.6 copy-start.2
  2.2 1.0 copy-start.7
  3.3 4.4 %copy-start.14 = (f32[1,1,128,2048]{3,2,1,0:T(8,128)S(1)}, f32[1,1,128,2048]{3,2,1,0:T(8,128)}, u32[]{:S(2)}) copy-start(f32[1,1,128,2048]{3,2,1,0:T(8,128)} %param.8) | copy-start | bytes 3145732
  4.5 8.6 %copy-start.20 = (s32[1,1,32]{2,1,0:T(1,128)S(1)}, s32[1,1,32]{2,1,0:T(1,128)}, u32[]{:S(2)}) copy-start(s32[1,1,32]{2,1,0:T(1,128)} %param.11) | copy-start | bytes 388
  4.5 9.0 %copy-start.3 = (bf16[1,1,1024,1024]{3,2,1,0:T(8,128)(2,1)S(1)}, bf16[1,1,1024,1024]{3,2,1,0:T(8,128)(2,1)}, u32[]{:S(2)}) copy-start(bf16[1,1,1024,1024]{3,2,1,0:T(8,128)(2,1)} %param.6) | copy-start | bytes 6291460
  4.5 9.0 %copy-start.8 = (bf16[1,1,1024,256]{3,2,1,0:T(8,128)(2,1)S(1)}, bf16[1,1,1024,256]{3,2,1,0:T(8,128)(2,1)}, u32[]{:S(2)}) copy-start(bf16[1,1,1024,256]{3,2,1,0:T(8,128)(2,1)} %param.9) | copy-start | bytes 1572868
  4.5 9.0 %collective-permute-start.2 = (s16[528,256]{1,0:T(8,128)(2,1)}, s16[528,256]{1,0:T(8,128)(2,1)}, u32[]{:S(2)}, u32[]{:S(2)}) collective-permute-start(s16[528,256]{1,0:T(8,128)(2,1)} %shard_map.81), channel_id=1, source_target_pairs={{1,0},{2,1},{3,2},{4,3},{5,4},{6,5},{7,6},{8,7},{9,8},{10,9},{11,1... | collective-permute-start | bytes 811016 | tf_op jit(solution)/shard_map/ppermute | solution.py:316
  8.9 10.7 %all-to-all-start = ((s16[4,144,512]{2,1,0:T(8,128)(2,1)}), s16[4,144,512]{2,1,0:T(8,128)(2,1)S(1)}, u32[]{:S(2)}, u32[]{:S(2)}) async-start(s16[4,144,512]{2,1,0:T(8,128)(2,1)} %shard_map.78), calls=%async_computation | async-start | bytes 1179648 | tf_op jit(solution)/shard_map/all_to_all | solution.py:320
  16.3 0.8 copy-start.15
  17.1 0.7 copy-start.17
  19.7 15.1 %copy-start.5 = (s16[4,144,512]{2,1,0:T(8,128)(2,1)}, s16[4,144,512]{2,1,0:T(8,128)(2,1)S(1)}, u32[]{:S(2)}) copy-start(s16[4,144,512]{2,1,0:T(8,128)(2,1)S(1)} %all-to-all-done.got_ref) | copy-start | bytes 1769476
  19.7 23.6 %all-to-all-start.1 = ((s16[16,72,128]{2,1,0:T(8,128)(2,1)}), s16[16,72,128]{2,1,0:T(8,128)(2,1)}, u32[]{:S(2)}, u32[]{:S(2)}) async-start(s16[16,72,128]{2,1,0:T(8,128)(2,1)} %copy-done.17), calls=%async_computation.1 | async-start | bytes 589824 | tf_op jit(solution)/shard_map/all_to_all | solution.py:320
  30.9 1.6 copy-start.4
  34.7 28.2 %collective-permute-start = (bf16[512,1024]{1,0:T(8,128)(2,1)}, bf16[512,1024]{1,0:T(8,128)(2,1)S(1)}, u32[]{:S(2)}, u32[]{:S(2)}) collective-permute-start(bf16[512,1024]{1,0:T(8,128)(2,1)} %get-tuple-element.36), channel_id=1, source_target_pairs={{1,0},{2,1},{3,2},{4,3},{5,4},{6,5},{7,6},{8,7},{9,8},{10,9},{11,1... | collective-permute-start | bytes 3145736 | tf_op jit(solution)/shard_map/ppermute | solution.py:316
  34.9 1.1 copy-start.6
  44.9 0.7 copy-start.13
  45.6 14.0 %all-to-all-start.2 = ((s16[16,72,128]{2,1,0:T(8,128)(2,1)}), s16[16,72,128]{2,1,0:T(8,128)(2,1)}, u32[]{:S(2)}, u32[]{:S(2)}) async-start(s16[16,72,128]{2,1,0:T(8,128)(2,1)} %copy-done.13), calls=%async_computation.2 | async-start | bytes 589824 | tf_op jit(solution)/shard_map/all_to_all | solution.py:320
  59.6 7.3 %copy-start.16 = (f32[512,256]{1,0:T(8,128)S(1)}, f32[512,256]{1,0:T(8,128)}, u32[]{:S(2)}) copy-start(f32[512,256]{1,0:T(8,128)} %copy-done.15) | copy-start | bytes 1572868
  61.0 6.7 %copy-start.9 = (f32[512,256]{1,0:T(8,128)}, f32[512,256]{1,0:T(8,128)S(1)}, u32[]{:S(2)}) copy-start(f32[512,256]{1,0:T(8,128)S(1)} %get-tuple-element.41.x_ref.dual_ref) | copy-start | bytes 1572868
  61.0 5.9 %collective-permute-start.4 = (bf16[512,256]{1,0:T(8,128)(2,1)S(1)}, bf16[512,256]{1,0:T(8,128)(2,1)S(1)}, u32[]{:S(2)}, u32[]{:S(2)}) collective-permute-start(bf16[512,256]{1,0:T(8,128)(2,1)S(1)} %get-tuple-element.40.xr_ref), channel_id=1, source_target_pairs={{1,0},{2,1},{3,2},{4,3},{5,4},{6,5},{7,6},{8,7},{9,8},{10,9},{11,1... | collective-permute-start | bytes 786440 | tf_op jit(solution)/shard_map/ppermute | solution.py:316
  62.1 4.8 %collective-permute-start.3 = (bf16[512,256]{1,0:T(8,128)(2,1)S(1)}, bf16[512,256]{1,0:T(8,128)(2,1)S(1)}, u32[]{:S(2)}, u32[]{:S(2)}) collective-permute-start(bf16[512,256]{1,0:T(8,128)(2,1)S(1)} %get-tuple-element.40.xr_ref), channel_id=1, source_target_pairs={{63,0},{0,1},{1,2},{2,3},{3,4},{4,5},{5,6},{6,7},{7,8},{8,9},{9,10... | collective-permute-start | bytes 786440 | tf_op jit(solution)/shard_map/ppermute | solution.py:316
  67.8 0.8 copy-start.11
  68.6 0.7 copy-start.18
  69.3 23.4 %all-to-all-start.3 = ((s16[16,72,128]{2,1,0:T(8,128)(2,1)}), s16[16,72,128]{2,1,0:T(8,128)(2,1)}, u32[]{:S(2)}, u32[]{:S(2)}) async-start(s16[16,72,128]{2,1,0:T(8,128)(2,1)} %copy-done.18), calls=%async_computation.3 | async-start | bytes 589824 | tf_op jit(solution)/shard_map/all_to_all | solution.py:320
  80.3 1.6 copy-start.19
  84.1 1.0 copy-start
  85.1 23.2 %collective-permute-start.1 = (bf16[512,1024]{1,0:T(8,128)(2,1)}, bf16[512,1024]{1,0:T(8,128)(2,1)}, u32[]{:S(2)}, u32[]{:S(2)}) collective-permute-start(bf16[512,1024]{1,0:T(8,128)(2,1)} %get-tuple-element.38), channel_id=1, source_target_pairs={{1,0},{2,1},{3,2},{4,3},{5,4},{6,5},{7,6},{8,7},{9,8},{10,9},{11,1... | collective-permute-start | bytes 3145736 | tf_op jit(solution)/shard_map/ppermute | solution.py:316
  92.7 13.4 %copy-start.12 = (f32[512,256]{1,0:T(8,128)S(1)}, f32[512,256]{1,0:T(8,128)}, u32[]{:S(2)}) copy-start(f32[512,256]{1,0:T(8,128)} %copy-done.11) | copy-start | bytes 1572868
  92.7 15.6 %copy-start.1 = (bf16[512,1024]{1,0:T(8,128)(2,1)S(1)}, bf16[512,1024]{1,0:T(8,128)(2,1)}, u32[]{:S(2)}) copy-start(bf16[512,1024]{1,0:T(8,128)(2,1)} %copy-done) | copy-start | bytes 3145732
  106.5 5.9 %collective-permute-start.6 = (bf16[512,256]{1,0:T(8,128)(2,1)S(1)}, bf16[512,256]{1,0:T(8,128)(2,1)S(1)}, u32[]{:S(2)}, u32[]{:S(2)}) collective-permute-start(bf16[512,256]{1,0:T(8,128)(2,1)S(1)} %get-tuple-element.45.xr_ref), channel_id=1, source_target_pairs={{1,0},{2,1},{3,2},{4,3},{5,4},{6,5},{7,6},{8,7},{9,8},{10,9},{11,1... | collective-permute-start | bytes 786440 | tf_op jit(solution)/shard_map/ppermute | solution.py:316
  107.5 4.8 %collective-permute-start.5 = (bf16[512,256]{1,0:T(8,128)(2,1)S(1)}, bf16[512,256]{1,0:T(8,128)(2,1)S(1)}, u32[]{:S(2)}, u32[]{:S(2)}) collective-permute-start(bf16[512,256]{1,0:T(8,128)(2,1)S(1)} %get-tuple-element.45.xr_ref), channel_id=1, source_target_pairs={{63,0},{0,1},{1,2},{2,3},{3,4},{4,5},{5,6},{6,7},{7,8},{8,9},{9,10... | collective-permute-start | bytes 786440 | tf_op jit(solution)/shard_map/ppermute | solution.py:316
  151.9 5.9 %collective-permute-start.8 = (bf16[512,256]{1,0:T(8,128)(2,1)S(1)}, bf16[512,256]{1,0:T(8,128)(2,1)S(1)}, u32[]{:S(2)}, u32[]{:S(2)}) collective-permute-start(bf16[512,256]{1,0:T(8,128)(2,1)S(1)} %get-tuple-element.49.xr_ref), channel_id=1, source_target_pairs={{1,0},{2,1},{3,2},{4,3},{5,4},{6,5},{7,6},{8,7},{9,8},{10,9},{11,1... | collective-permute-start | bytes 786440 | tf_op jit(solution)/shard_map/ppermute | solution.py:316
  152.9 4.8 %collective-permute-start.7 = (bf16[512,256]{1,0:T(8,128)(2,1)S(1)}, bf16[512,256]{1,0:T(8,128)(2,1)S(1)}, u32[]{:S(2)}, u32[]{:S(2)}) collective-permute-start(bf16[512,256]{1,0:T(8,128)(2,1)S(1)} %get-tuple-element.49.xr_ref), channel_id=1, source_target_pairs={{63,0},{0,1},{1,2},{2,3},{3,4},{4,5},{5,6},{6,7},{7,8},{8,9},{9,10... | collective-permute-start | bytes 786440 | tf_op jit(solution)/shard_map/ppermute | solution.py:316
  158.6 32.4 %copy-start.10 = (f32[512,256]{1,0:T(8,128)S(1)}, f32[512,256]{1,0:T(8,128)}, u32[]{:S(2)}) copy-start(f32[512,256]{1,0:T(8,128)} %copy-done.9) | copy-start | bytes 1572868
  191.5 5.9 %collective-permute-start.10 = (bf16[512,256]{1,0:T(8,128)(2,1)S(1)}, bf16[512,256]{1,0:T(8,128)(2,1)S(1)}, u32[]{:S(2)}, u32[]{:S(2)}) collective-permute-start(bf16[512,256]{1,0:T(8,128)(2,1)S(1)} %get-tuple-element.55.xr_ref), channel_id=1, source_target_pairs={{1,0},{2,1},{3,2},{4,3},{5,4},{6,5},{7,6},{8,7},{9,8},{10,9},{11,1... | collective-permute-start | bytes 786440 | tf_op jit(solution)/shard_map/ppermute | solution.py:316
  192.5 4.8 %collective-permute-start.9 = (bf16[512,256]{1,0:T(8,128)(2,1)S(1)}, bf16[512,256]{1,0:T(8,128)(2,1)S(1)}, u32[]{:S(2)}, u32[]{:S(2)}) collective-permute-start(bf16[512,256]{1,0:T(8,128)(2,1)S(1)} %get-tuple-element.55.xr_ref), channel_id=1, source_target_pairs={{63,0},{0,1},{1,2},{2,3},{3,4},{4,5},{5,6},{6,7},{7,8},{8,9},{9,10... | collective-permute-start | bytes 786440 | tf_op jit(solution)/shard_map/ppermute | solution.py:316
  232.0 5.9 %collective-permute-start.12 = (bf16[512,256]{1,0:T(8,128)(2,1)S(1)}, bf16[512,256]{1,0:T(8,128)(2,1)S(1)}, u32[]{:S(2)}, u32[]{:S(2)}) collective-permute-start(bf16[512,256]{1,0:T(8,128)(2,1)S(1)} %get-tuple-element.59.xr_ref), channel_id=1, source_target_pairs={{1,0},{2,1},{3,2},{4,3},{5,4},{6,5},{7,6},{8,7},{9,8},{10,9},{11,1... | collective-permute-start | bytes 786440 | tf_op jit(solution)/shard_map/ppermute | solution.py:316
  233.1 4.8 %collective-permute-start.11 = (bf16[512,256]{1,0:T(8,128)(2,1)S(1)}, bf16[512,256]{1,0:T(8,128)(2,1)S(1)}, u32[]{:S(2)}, u32[]{:S(2)}) collective-permute-start(bf16[512,256]{1,0:T(8,128)(2,1)S(1)} %get-tuple-element.59.xr_ref), channel_id=1, source_target_pairs={{63,0},{0,1},{1,2},{2,3},{3,4},{4,5},{5,6},{6,7},{7,8},{8,9},{9,10... | collective-permute-start | bytes 786440 | tf_op jit(solution)/shard_map/ppermute | solution.py:316

commit v2 on v1

--- a/solution.py
+++ b/solution.py
@@ -159,18 +159,27 @@
     away_ref[:, reach:] = mm(mat_ref[0:reach, reach:], flip).astype(BF16)
 
 
-def tile_kernel(near, far, tile_ref, out_ref):
+def tile_kernel(near, far, place_ref, tile_ref, out_ref, *rest):
+    *away_refs, all_ref = rest
+    place = place_ref[0, 0]
     waves = tile_ref.shape[1] // (near * far)
     value = tile_ref[...]
     for j in range(near):
         pieces = [value[:, (k * near + j) * waves : (k * near + j + 1) * waves] for k in range(far)]
-        coded(jnp.concatenate(pieces, axis=1), out_ref.at[j])
-
-
-def parts_kernel(got_ref, out_ref):
+        coded(jnp.concatenate(pieces, axis=1), all_ref.at[lax.rem(j + near - place, near)])
+    for d, ref in enumerate((out_ref, *away_refs)):
+        ref[...] = all_ref[d]
+
+
+def parts_kernel(place_ref, *refs):
+    *got_refs, out_ref = refs
+    near = len(got_refs)
     rows = out_ref.shape[1] // 2
-    for j in range(got_ref.shape[0]):
-        out_ref[j, 0:rows], out_ref[j, rows:] = halves(decoded(got_ref.at[j]))
+    for d, ref in enumerate(got_refs):
+        source = lax.rem(place_ref[0, 0] + near - d, near)
+        high, low = halves(decoded(ref))
+        out_ref[source, 0:rows] = high
+        out_ref[source, rows:] = low
 
 
 def rhs_kernel(size_ref, mat_ref, loads_ref, heads_ref, wt_hi, wt_lo, rhs_ref, pay_ref):
@@ -336,15 +345,29 @@
 
     heads, = call(heads_kernel, [((reach + 16, columns), jnp.int16)], 2 * reach * width * columns, 2 << 20)(nmat, load)
     heads = passed_along(heads, -1)
-    spread, = call(
+    place = lax.axis_index("x").astype(jnp.int32).reshape(1, 1)
+    smem = pl.BlockSpec(memory_space=pltpu.SMEM)
+    vmem = pl.BlockSpec(memory_space=pltpu.VMEM)
+    block = ((tile.shape[0] + 16, tile.shape[1] // near), jnp.int16)
+    kept, *sent = pl.pallas_call(
         functools.partial(tile_kernel, near, lax.axis_size("z")),
-        [((near, tile.shape[0] + 16, tile.shape[1] // near), jnp.int16)],
-        size=2 << 20,
-    )(tile)
-    tiles = exchange(spread, "x")
-    tiles, = call(
-        parts_kernel, [((near, 2 * tile.shape[0], tile.shape[1] // near), BF16)], size=2 << 20
-    )(tiles)
+        out_shape=[jax.ShapeDtypeStruct(*block)] * near,
+        in_specs=[smem, vmem],
+        scratch_shapes=[pltpu.VMEM((near, *block[0]), block[1])],
+        name="tile",
+        compiler_params=GRANT,
+    )(place, tile)
+    came = [
+        lax.ppermute(sent[d - 1], "x", [(i, (i + d) % near) for i in range(near)])
+        for d in range(1, near)
+    ]
+    tiles = pl.pallas_call(
+        parts_kernel,
+        out_shape=jax.ShapeDtypeStruct((near, 2 * tile.shape[0], tile.shape[1] // near), BF16),
+        in_specs=[smem] + [vmem] * near,
+        name="parts",
+        compiler_params=GRANT,
+    )(place, kept, *came)
     turn = call(turn_kernel, [((reach, width), BF16)] * 2, 6 * reach**3, 4 << 20)
     n_own, n_away = turn(nmat)
     n_away = passed_along(n_away, -1)

time: 265 us -> 275 us (1.038)
  waiting for transfers between devices: 40 us -> 50.3 us
  starting transfers between devices: 43.2 us -> 46.6 us
    ppermute x0 -> x3, waiting for transfers between devices: none -> 17.5 us  [shards(): lax.ppermute(sent[d - 1], 'x', [(i, (i + d) % near) for i in range(near)])]
    all_to_all x4 -> x3, waiting for transfers between devices: 24.4 us -> 14.8 us  [exchange(): return lax.all_to_all(value, axes, 0, 0, tiled=True)]
    ppermute x0 -> x3, starting transfers between devices: none -> 4.12 us  [shards(): lax.ppermute(sent[d - 1], 'x', [(i, (i + d) % near) for i in range(near)])]
    unnamed x42 -> x32, local copies, waits for them, and re-layouts: 11.6 us -> 9.8 us
    all_to_all x4 -> x3, starting transfers between devices: 30.6 us -> 29.6 us  [exchange(): return lax.all_to_all(value, axes, 0, 0, tiled=True)]
  transfers between devices with their start and end apart: 17 -> 19, of which waited for: 9 -> 11; matrix products, arithmetic and copies ran while one was open for 1% -> 0% of each run, Pallas kernels for 7% -> 5%
where the time goes in v2:
time: 275 us; the launch traced here: 274 us
  blocking collectives  136 us (49%)
  waiting for transfers between devices  50.3 us (18%)
  starting transfers between devices  46.6 us (17%)
  Pallas kernels  29 us (11%)
  local copies, waits for them, and re-layouts  9.8 us (4%)
    all_to_all x9, blocking collectives, exchange(): return lax.all_to_all(value, axes, 0, 0, tiled=True)  136 us
    all_to_all x3, starting transfers between devices, exchange(): return lax.all_to_all(value, axes, 0, 0, tiled=True)  29.6 us
    ppermute x13, waiting for transfers between devices, passed_along(): return lax.ppermute(block, SUB, [((i - distance) % n, i) for i in range(n)])  18 us
    ppermute x3, waiting for transfers between devices, shards(): lax.ppermute(sent[d - 1], 'x', [(i, (i + d) % near) for i in range(near)])  17.5 us
    all_to_all x3, waiting for transfers between devices, exchange(): return lax.all_to_all(value, axes, 0, 0, tiled=True)  14.8 us
    ppermute x13, starting transfers between devices, passed_along(): return lax.ppermute(block, SUB, [((i - distance) % n, i) for i in range(n)])  13 us
    unnamed x32, local copies, waits for them, and re-layouts  9.8 us
    pallas_call x5, Pallas kernels, apply(): pl.pallas_call(functools.partial(apply_kernel, mode), out_shape=[jax.Shap...  6.23 us
  transfers between devices with their start and end apart: 19, of which 11 were waited for; matrix products, arithmetic and copies ran while one was open for 0% of the time, Pallas kernels for 5%

profile of v2, /device:TPU:1, one launch (start us, length us, event | category | flops | bytes accessed | tf_op | source)
XLA Modules:
  0.0 274.2 jit_solution(11736302126682156637)
XLA Ops:
  0.7 1.6 copy-done.2
  2.2 1.0 copy-done.4
  3.8 3.3 %collective-permute-start.5 = (s16[528,256]{1,0:T(8,128)(2,1)S(1)}, s16[528,256]{1,0:T(8,128)(2,1)S(1)}, u32[]{:S(2)}, u32[]{:S(2)}) collective-permute-start(s16[528,256]{1,0:T(8,128)(2,1)S(1)} %shard_map.79), channel_id=1, source_target_pairs={{1,0},{2,1},{3,2},{4,3},{5,4},{6,5},{7,6},{8,7},{9,8},{10,9},{11,1... | collective-permute-start | bytes 811016 | tf_op jit(solution)/shard_map/ppermute | solution.py:325
  8.1 2.5 collective-permute-done.5.heads_ref
  10.6 2.6 rhs.1
  14.0 10.2 %all-to-all-start = ((s16[16,72,128]{2,1,0:T(8,128)(2,1)}), s16[16,72,128]{2,1,0:T(8,128)(2,1)}, u32[]{:S(2)}, u32[]{:S(2)}) async-start(s16[16,72,128]{2,1,0:T(8,128)(2,1)} %get-tuple-element.47), calls=%async_computation | async-start | bytes 589824 | tf_op jit(solution)/shard_map/all_to_all | solution.py:329
  24.1 1.6 copy-done.3
  25.7 2.3 shard_map.77
  28.8 4.0 %collective-permute-start.2 = (s16[144,512]{1,0:T(8,128)(2,1)S(1)}, s16[144,512]{1,0:T(8,128)(2,1)S(1)}, u32[]{:S(2)}, u32[]{:S(2)}) collective-permute-start(s16[144,512]{1,0:T(8,128)(2,1)S(1)} %get-tuple-element.43), channel_id=1, source_target_pairs={{0,4},{2,6},{4,0},{6,2},{1,5},{3,7},{5,1},{7,3},{8,12},{10,14},{12... | collective-permute-start | bytes 442376 | tf_op jit(solution)/shard_map/ppermute | solution.py:361
  32.8 1.7 collective-permute-done.1.refs_1_
  34.6 4.0 %collective-permute-done.2.refs_2_ = s16[144,512]{1,0:T(8,128)(2,1)S(1)} collective-permute-done((s16[144,512]{1,0:T(8,128)(2,1)S(1)}, s16[144,512]{1,0:T(8,128)(2,1)S(1)}, u32[]{:S(2)}, u32[]{:S(2)}) %collective-permute-start.2) | collective-permute-done | bytes 147488 | tf_op jit(solution)/shard_map/ppermute | solution.py:361
  38.5 11.8 %collective-permute-done.3.refs_3_ = s16[144,512]{1,0:T(8,128)(2,1)S(1)} collective-permute-done((s16[144,512]{1,0:T(8,128)(2,1)S(1)}, s16[144,512]{1,0:T(8,128)(2,1)S(1)}, u32[]{:S(2)}, u32[]{:S(2)}) %collective-permute-start.3) | collective-permute-done | bytes 147488 | tf_op jit(solution)/shard_map/ppermute | solution.py:361
  50.6 1.6 shard_map.80
  52.9 7.5 %all-to-all-start.1 = ((s16[16,72,128]{2,1,0:T(8,128)(2,1)}), s16[16,72,128]{2,1,0:T(8,128)(2,1)}, u32[]{:S(2)}, u32[]{:S(2)}) async-start(s16[16,72,128]{2,1,0:T(8,128)(2,1)} %copy-done.9), calls=%async_computation.1 | async-start | bytes 589824 | tf_op jit(solution)/shard_map/all_to_all | solution.py:329
  60.4 1.0 fusion
  61.4 7.4 %all-to-all-done.1.got_ref = s16[16,72,128]{2,1,0:T(8,128)(2,1)} async-done(((s16[16,72,128]{2,1,0:T(8,128)(2,1)}), s16[16,72,128]{2,1,0:T(8,128)(2,1)}, u32[]{:S(2)}, u32[]{:S(2)}) %all-to-all-start.1) | async-done | bytes 294944 | tf_op jit(solution)/shard_map/all_to_all | solution.py:329
  68.8 1.4 shard_map.81
  70.3 1.7 collective-permute-start.7
  72.7 3.5 %collective-permute-done.7.next_ref = bf16[512,256]{1,0:T(8,128)(2,1)S(1)} collective-permute-done((bf16[512,256]{1,0:T(8,128)(2,1)S(1)}, bf16[512,256]{1,0:T(8,128)(2,1)S(1)}, u32[]{:S(2)}, u32[]{:S(2)}) %collective-permute-start.7) | collective-permute-done | bytes 262176 | tf_op jit(solution)/shard_map/ppermute | solution.py:325
  78.6 11.9 %all-to-all-start.2 = ((s16[16,72,128]{2,1,0:T(8,128)(2,1)}), s16[16,72,128]{2,1,0:T(8,128)(2,1)}, u32[]{:S(2)}, u32[]{:S(2)}) async-start(s16[16,72,128]{2,1,0:T(8,128)(2,1)} %copy-done.13), calls=%async_computation.2 | async-start | bytes 589824 | tf_op jit(solution)/shard_map/all_to_all | solution.py:329
  90.5 1.6 copy-done.14
  92.1 2.3 shard_map.78
  94.3 1.0 copy-done
  95.5 7.4 %all-to-all-done.2.got_ref = s16[16,72,128]{2,1,0:T(8,128)(2,1)} async-done(((s16[16,72,128]{2,1,0:T(8,128)(2,1)}), s16[16,72,128]{2,1,0:T(8,128)(2,1)}, u32[]{:S(2)}, u32[]{:S(2)}) %all-to-all-start.2) | async-done | bytes 294944 | tf_op jit(solution)/shard_map/all_to_all | solution.py:329
  102.9 1.8 shard_map.84
  104.7 12.2 %all_to_all.60.got_ref = s16[16,72,128]{2,1,0:T(8,128)(2,1)S(1)} all-to-all(s16[16,72,128]{2,1,0:T(8,128)(2,1)S(1)} %shard_map.84), channel_id=1, replica_groups=mesh['grp'=4,'z'=8,'x'=4,'c'=2] {'grp','x'}, dimensions={0} | all-to-all | bytes 589824 | tf_op jit(solution)/shard_map/all_to_all | solution.py:329
  117.8 1.3 collective-permute-start.8
  119.1 1.7 shard_map.86.inner_ref
  120.8 2.4 collective-permute-done.9.next_ref
  123.2 2.1 shard_map.87
  125.2 23.0 %all_to_all.61.got_ref = s16[16,72,128]{2,1,0:T(8,128)(2,1)S(1)} all-to-all(s16[16,72,128]{2,1,0:T(8,128)(2,1)S(1)} %get-tuple-element.55), channel_id=1, replica_groups=mesh['grp'=4,'z'=8,'x'=4,'c'=2] {'z','c'}, dimensions={0} | all-to-all | bytes 589824 | tf_op jit(solution)/shard_map/all_to_all | solution.py:329
  149.0 12.7 %all_to_all.62.got_ref = s16[16,72,128]{2,1,0:T(8,128)(2,1)S(1)} all-to-all(s16[16,72,128]{2,1,0:T(8,128)(2,1)S(1)} %shard_map.88), channel_id=1, replica_groups=mesh['grp'=4,'z'=8,'x'=4,'c'=2] {'grp','x'}, dimensions={0} | all-to-all | bytes 589824 | tf_op jit(solution)/shard_map/all_to_all | solution.py:329
  162.1 1.1 collective-permute-start.11
  164.4 3.6 %collective-permute-done.11.next_ref = bf16[512,256]{1,0:T(8,128)(2,1)S(1)} collective-permute-done((bf16[512,256]{1,0:T(8,128)(2,1)S(1)}, bf16[512,256]{1,0:T(8,128)(2,1)S(1)}, u32[]{:S(2)}, u32[]{:S(2)}) %collective-permute-start.11) | collective-permute-done | bytes 262176 | tf_op jit(solution)/shard_map/ppermute | solution.py:325
  168.0 0.8 shard_map.91
  168.8 19.8 %all_to_all.63.got_ref = s16[16,72,128]{2,1,0:T(8,128)(2,1)S(1)} all-to-all(s16[16,72,128]{2,1,0:T(8,128)(2,1)S(1)} %get-tuple-element.59), channel_id=1, replica_groups=mesh['grp'=4,'z'=8,'x'=4,'c'=2] {'z','c'}, dimensions={0} | all-to-all | bytes 589824 | tf_op jit(solution)/shard_map/all_to_all | solution.py:329
  189.4 11.8 %all_to_all.64.got_ref = s16[16,72,128]{2,1,0:T(8,128)(2,1)S(1)} all-to-all(s16[16,72,128]{2,1,0:T(8,128)(2,1)S(1)} %shard_map.92), channel_id=1, replica_groups=mesh['grp'=4,'z'=8,'x'=4,'c'=2] {'grp','x'}, dimensions={0} | all-to-all | bytes 589824 | tf_op jit(solution)/shard_map/all_to_all | solution.py:329
  201.7 1.1 collective-permute-start.13
  203.5 1.7 shard_map.94.inner_ref
  205.2 2.4 collective-permute-done.13.next_ref
  207.6 2.1 shard_map.95
  209.6 19.7 %all_to_all.65.got_ref = s16[16,72,128]{2,1,0:T(8,128)(2,1)S(1)} all-to-all(s16[16,72,128]{2,1,0:T(8,128)(2,1)S(1)} %get-tuple-element.65), channel_id=1, replica_groups=mesh['grp'=4,'z'=8,'x'=4,'c'=2] {'z','c'}, dimensions={0} | all-to-all | bytes 589824 | tf_op jit(solution)/shard_map/all_to_all | solution.py:329
  230.1 11.8 %all_to_all.66.got_ref = s16[16,72,128]{2,1,0:T(8,128)(2,1)S(1)} all-to-all(s16[16,72,128]{2,1,0:T(8,128)(2,1)S(1)} %shard_map.96), channel_id=1, replica_groups=mesh['grp'=4,'z'=8,'x'=4,'c'=2] {'grp','x'}, dimensions={0} | all-to-all | bytes 589824 | tf_op jit(solution)/shard_map/all_to_all | solution.py:329
  242.3 1.1 collective-permute-start.15
  244.5 3.6 %collective-permute-done.15.next_ref = bf16[512,256]{1,0:T(8,128)(2,1)S(1)} collective-permute-done((bf16[512,256]{1,0:T(8,128)(2,1)S(1)}, bf16[512,256]{1,0:T(8,128)(2,1)S(1)}, u32[]{:S(2)}, u32[]{:S(2)}) %collective-permute-start.15) | collective-permute-done | bytes 262176 | tf_op jit(solution)/shard_map/ppermute | solution.py:325
  248.6 15.2 %all_to_all.67.got_ref = f32[16,8,128]{2,1,0:T(8,128)S(1)} all-to-all(f32[16,8,128]{2,1,0:T(8,128)S(1)} %get-tuple-element.69), channel_id=1, replica_groups=mesh['grp'=4,'z'=8,'x'=4,'c'=2] {'z','c'}, dimensions={0} | all-to-all | bytes 131072 | tf_op jit(solution)/shard_map/all_to_all | solution.py:329
  263.8 9.3 %all_to_all.68.got_ref = f32[16,8,128]{2,1,0:T(8,128)S(1)} all-to-all(f32[16,8,128]{2,1,0:T(8,128)S(1)} %shard_map.100), channel_id=1, replica_groups=mesh['grp'=4,'z'=8,'x'=4,'c'=2] {'grp','x'}, dimensions={0} | all-to-all | bytes 131072 | tf_op jit(solution)/shard_map/all_to_all | solution.py:329
  273.2 1.1 shard_map.101
  (65 shorter events, 14.6 us)
Async XLA Ops:
  0.6 7.1 %copy-start.15 = (s32[1,1,32]{2,1,0:T(1,128)S(1)}, s32[1,1,32]{2,1,0:T(1,128)}, u32[]{:S(2)}) copy-start(s32[1,1,32]{2,1,0:T(1,128)} %param.11) | copy-start | bytes 388
  0.6 1.6 copy-start.2
  2.2 1.0 copy-start.4
  3.8 6.8 %collective-permute-start.5 = (s16[528,256]{1,0:T(8,128)(2,1)S(1)}, s16[528,256]{1,0:T(8,128)(2,1)S(1)}, u32[]{:S(2)}, u32[]{:S(2)}) collective-permute-start(s16[528,256]{1,0:T(8,128)(2,1)S(1)} %shard_map.79), channel_id=1, source_target_pairs={{1,0},{2,1},{3,2},{4,3},{5,4},{6,5},{7,6},{8,7},{9,8},{10,9},{11,1... | collective-permute-start | bytes 811016 | tf_op jit(solution)/shard_map/ppermute | solution.py:325
  10.6 17.7 %copy-start.10 = (f32[1,1,128,2048]{3,2,1,0:T(8,128)S(1)}, f32[1,1,128,2048]{3,2,1,0:T(8,128)}, u32[]{:S(2)}) copy-start(f32[1,1,128,2048]{3,2,1,0:T(8,128)} %param.8) | copy-start | bytes 3145732
  13.2 0.8 copy-start.11
  14.0 36.6 %all-to-all-start = ((s16[16,72,128]{2,1,0:T(8,128)(2,1)}), s16[16,72,128]{2,1,0:T(8,128)(2,1)}, u32[]{:S(2)}, u32[]{:S(2)}) async-start(s16[16,72,128]{2,1,0:T(8,128)(2,1)} %get-tuple-element.47), calls=%async_computation | async-start | bytes 589824 | tf_op jit(solution)/shard_map/all_to_all | solution.py:329
  24.1 1.6 copy-start.3
  28.0 44.3 %collective-permute-start = (bf16[512,1024]{1,0:T(8,128)(2,1)}, bf16[512,1024]{1,0:T(8,128)(2,1)S(1)}, u32[]{:S(2)}, u32[]{:S(2)}) collective-permute-start(bf16[512,1024]{1,0:T(8,128)(2,1)} %get-tuple-element.40), channel_id=1, source_target_pairs={{1,0},{2,1},{3,2},{4,3},{5,4},{6,5},{7,6},{8,7},{9,8},{10,9},{11,1... | collective-permute-start | bytes 3145736 | tf_op jit(solution)/shard_map/ppermute | solution.py:325
  28.7 5.9 %collective-permute-start.1 = (s16[144,512]{1,0:T(8,128)(2,1)S(1)}, s16[144,512]{1,0:T(8,128)(2,1)S(1)}, u32[]{:S(2)}, u32[]{:S(2)}) collective-permute-start(s16[144,512]{1,0:T(8,128)(2,1)S(1)} %get-tuple-element.42), channel_id=1, source_target_pairs={{0,2},{2,4},{4,6},{6,0},{1,3},{3,5},{5,7},{7,1},{8,10},{10,12},{12... | collective-permute-start | bytes 442376 | tf_op jit(solution)/shard_map/ppermute | solution.py:361
  28.8 9.7 %collective-permute-start.2 = (s16[144,512]{1,0:T(8,128)(2,1)S(1)}, s16[144,512]{1,0:T(8,128)(2,1)S(1)}, u32[]{:S(2)}, u32[]{:S(2)}) collective-permute-start(s16[144,512]{1,0:T(8,128)(2,1)S(1)} %get-tuple-element.43), channel_id=1, source_target_pairs={{0,4},{2,6},{4,0},{6,2},{1,5},{3,7},{5,1},{7,3},{8,12},{10,14},{12... | collective-permute-start | bytes 442376 | tf_op jit(solution)/shard_map/ppermute | solution.py:361
  32.8 17.5 %collective-permute-start.3 = (s16[144,512]{1,0:T(8,128)(2,1)S(1)}, s16[144,512]{1,0:T(8,128)(2,1)S(1)}, u32[]{:S(2)}, u32[]{:S(2)}) collective-permute-start(s16[144,512]{1,0:T(8,128)(2,1)S(1)} %get-tuple-element.44), channel_id=1, source_target_pairs={{0,6},{2,0},{4,2},{6,4},{1,7},{3,1},{5,3},{7,5},{8,14},{10,8},{12,... | collective-permute-start | bytes 442376 | tf_op jit(solution)/shard_map/ppermute | solution.py:361
  52.2 0.7 copy-start.9
  52.9 15.9 %all-to-all-start.1 = ((s16[16,72,128]{2,1,0:T(8,128)(2,1)}), s16[16,72,128]{2,1,0:T(8,128)(2,1)}, u32[]{:S(2)}, u32[]{:S(2)}) async-start(s16[16,72,128]{2,1,0:T(8,128)(2,1)} %copy-done.9), calls=%async_computation.1 | async-start | bytes 589824 | tf_op jit(solution)/shard_map/all_to_all | solution.py:329
  68.8 7.4 %copy-start.12 = (f32[512,256]{1,0:T(8,128)S(1)}, f32[512,256]{1,0:T(8,128)}, u32[]{:S(2)}) copy-start(f32[512,256]{1,0:T(8,128)} %copy-done.11) | copy-start | bytes 1572868
  70.3 6.8 %copy-start.5 = (f32[512,256]{1,0:T(8,128)}, f32[512,256]{1,0:T(8,128)S(1)}, u32[]{:S(2)}) copy-start(f32[512,256]{1,0:T(8,128)S(1)} %get-tuple-element.49.x_ref.dual_ref) | copy-start | bytes 1572868
  70.3 5.9 %collective-permute-start.7 = (bf16[512,256]{1,0:T(8,128)(2,1)S(1)}, bf16[512,256]{1,0:T(8,128)(2,1)S(1)}, u32[]{:S(2)}, u32[]{:S(2)}) collective-permute-start(bf16[512,256]{1,0:T(8,128)(2,1)S(1)} %get-tuple-element.48.xr_ref), channel_id=1, source_target_pairs={{1,0},{2,1},{3,2},{4,3},{5,4},{6,5},{7,6},{8,7},{9,8},{10,9},{11,1... | collective-permute-start | bytes 786440 | tf_op jit(solution)/shard_map/ppermute | solution.py:325
  72.0 4.2 %collective-permute-start.6 = (bf16[512,256]{1,0:T(8,128)(2,1)S(1)}, bf16[512,256]{1,0:T(8,128)(2,1)S(1)}, u32[]{:S(2)}, u32[]{:S(2)}) collective-permute-start(bf16[512,256]{1,0:T(8,128)(2,1)S(1)} %get-tuple-element.48.xr_ref), channel_id=1, source_target_pairs={{63,0},{0,1},{1,2},{2,3},{3,4},{4,5},{5,6},{6,7},{7,8},{8,9},{9,10... | collective-permute-start | bytes 786440 | tf_op jit(solution)/shard_map/ppermute | solution.py:325
  77.1 0.8 copy-start.7
  77.9 0.7 copy-start.13
  78.6 24.3 %all-to-all-start.2 = ((s16[16,72,128]{2,1,0:T(8,128)(2,1)}), s16[16,72,128]{2,1,0:T(8,128)(2,1)}, u32[]{:S(2)}, u32[]{:S(2)}) async-start(s16[16,72,128]{2,1,0:T(8,128)(2,1)} %copy-done.13), calls=%async_computation.2 | async-start | bytes 589824 | tf_op jit(solution)/shard_map/all_to_all | solution.py:329
  90.5 1.6 copy-start.14
  94.3 1.0 copy-start
  95.3 23.8 %collective-permute-start.4 = (bf16[512,1024]{1,0:T(8,128)(2,1)}, bf16[512,1024]{1,0:T(8,128)(2,1)}, u32[]{:S(2)}, u32[]{:S(2)}) collective-permute-start(bf16[512,1024]{1,0:T(8,128)(2,1)} %get-tuple-element.46), channel_id=1, source_target_pairs={{1,0},{2,1},{3,2},{4,3},{5,4},{6,5},{7,6},{8,7},{9,8},{10,9},{11,1... | collective-permute-start | bytes 3145736 | tf_op jit(solution)/shard_map/ppermute | solution.py:325
  102.9 14.0 %copy-start.8 = (f32[512,256]{1,0:T(8,128)S(1)}, f32[512,256]{1,0:T(8,128)}, u32[]{:S(2)}) copy-start(f32[512,256]{1,0:T(8,128)} %copy-done.7) | copy-start | bytes 1572868
  102.9 16.2 %copy-start.1 = (bf16[512,1024]{1,0:T(8,128)(2,1)S(1)}, bf16[512,1024]{1,0:T(8,128)(2,1)}, u32[]{:S(2)}) copy-start(bf16[512,1024]{1,0:T(8,128)(2,1)} %copy-done) | copy-start | bytes 3145732
  117.3 5.9 %collective-permute-start.9 = (bf16[512,256]{1,0:T(8,128)(2,1)S(1)}, bf16[512,256]{1,0:T(8,128)(2,1)S(1)}, u32[]{:S(2)}, u32[]{:S(2)}) collective-permute-start(bf16[512,256]{1,0:T(8,128)(2,1)S(1)} %get-tuple-element.53.xr_ref), channel_id=1, source_target_pairs={{1,0},{2,1},{3,2},{4,3},{5,4},{6,5},{7,6},{8,7},{9,8},{10,9},{11,1... | collective-permute-start | bytes 786440 | tf_op jit(solution)/shard_map/ppermute | solution.py:325
  117.8 5.4 %collective-permute-start.8 = (bf16[512,256]{1,0:T(8,128)(2,1)S(1)}, bf16[512,256]{1,0:T(8,128)(2,1)S(1)}, u32[]{:S(2)}, u32[]{:S(2)}) collective-permute-start(bf16[512,256]{1,0:T(8,128)(2,1)S(1)} %get-tuple-element.53.xr_ref), channel_id=1, source_target_pairs={{63,0},{0,1},{1,2},{2,3},{3,4},{4,5},{5,6},{6,7},{7,8},{8,9},{9,10... | collective-permute-start | bytes 786440 | tf_op jit(solution)/shard_map/ppermute | solution.py:325
  162.1 5.9 %collective-permute-start.11 = (bf16[512,256]{1,0:T(8,128)(2,1)S(1)}, bf16[512,256]{1,0:T(8,128)(2,1)S(1)}, u32[]{:S(2)}, u32[]{:S(2)}) collective-permute-start(bf16[512,256]{1,0:T(8,128)(2,1)S(1)} %get-tuple-element.57.xr_ref), channel_id=1, source_target_pairs={{1,0},{2,1},{3,2},{4,3},{5,4},{6,5},{7,6},{8,7},{9,8},{10,9},{11,1... | collective-permute-start | bytes 786440 | tf_op jit(solution)/shard_map/ppermute | solution.py:325
  163.2 4.8 %collective-permute-start.10 = (bf16[512,256]{1,0:T(8,128)(2,1)S(1)}, bf16[512,256]{1,0:T(8,128)(2,1)S(1)}, u32[]{:S(2)}, u32[]{:S(2)}) collective-permute-start(bf16[512,256]{1,0:T(8,128)(2,1)S(1)} %get-tuple-element.57.xr_ref), channel_id=1, source_target_pairs={{63,0},{0,1},{1,2},{2,3},{3,4},{4,5},{5,6},{6,7},{7,8},{8,9},{9,10... | collective-permute-start | bytes 786440 | tf_op jit(solution)/shard_map/ppermute | solution.py:325
  168.8 32.3 %copy-start.6 = (f32[512,256]{1,0:T(8,128)S(1)}, f32[512,256]{1,0:T(8,128)}, u32[]{:S(2)}) copy-start(f32[512,256]{1,0:T(8,128)} %copy-done.5) | copy-start | bytes 1572868
  201.7 5.9 %collective-permute-start.13 = (bf16[512,256]{1,0:T(8,128)(2,1)S(1)}, bf16[512,256]{1,0:T(8,128)(2,1)S(1)}, u32[]{:S(2)}, u32[]{:S(2)}) collective-permute-start(bf16[512,256]{1,0:T(8,128)(2,1)S(1)} %get-tuple-element.63.xr_ref), channel_id=1, source_target_pairs={{1,0},{2,1},{3,2},{4,3},{5,4},{6,5},{7,6},{8,7},{9,8},{10,9},{11,1... | collective-permute-start | bytes 786440 | tf_op jit(solution)/shard_map/ppermute | solution.py:325
  202.8 4.8 %collective-permute-start.12 = (bf16[512,256]{1,0:T(8,128)(2,1)S(1)}, bf16[512,256]{1,0:T(8,128)(2,1)S(1)}, u32[]{:S(2)}, u32[]{:S(2)}) collective-permute-start(bf16[512,256]{1,0:T(8,128)(2,1)S(1)} %get-tuple-element.63.xr_ref), channel_id=1, source_target_pairs={{63,0},{0,1},{1,2},{2,3},{3,4},{4,5},{5,6},{6,7},{7,8},{8,9},{9,10... | collective-permute-start | bytes 786440 | tf_op jit(solution)/shard_map/ppermute | solution.py:325
  242.3 5.9 %collective-permute-start.15 = (bf16[512,256]{1,0:T(8,128)(2,1)S(1)}, bf16[512,256]{1,0:T(8,128)(2,1)S(1)}, u32[]{:S(2)}, u32[]{:S(2)}) collective-permute-start(bf16[512,256]{1,0:T(8,128)(2,1)S(1)} %get-tuple-element.67.xr_ref), channel_id=1, source_target_pairs={{1,0},{2,1},{3,2},{4,3},{5,4},{6,5},{7,6},{8,7},{9,8},{10,9},{11,1... | collective-permute-start | bytes 786440 | tf_op jit(solution)/shard_map/ppermute | solution.py:325
  243.4 4.8 %collective-permute-start.14 = (bf16[512,256]{1,0:T(8,128)(2,1)S(1)}, bf16[512,256]{1,0:T(8,128)(2,1)S(1)}, u32[]{:S(2)}, u32[]{:S(2)}) collective-permute-start(bf16[512,256]{1,0:T(8,128)(2,1)S(1)} %get-tuple-element.67.xr_ref), channel_id=1, source_target_pairs={{63,0},{0,1},{1,2},{2,3},{3,4},{4,5},{5,6},{6,7},{7,8},{8,9},{9,10... | collective-permute-start | bytes 786440 | tf_op jit(solution)/shard_map/ppermute | solution.py:325

commit v3 on v2

--- a/solution.py
+++ b/solution.py
@@ -184,13 +184,8 @@
 
 def rhs_kernel(size_ref, mat_ref, loads_ref, heads_ref, wt_hi, wt_lo, rhs_ref, pay_ref):
     reach = rhs_ref.shape[0]
-    low = mm(mat_ref[reach:], loads_ref[...])
-    flip = reversal(reach)
-    high_part = low.astype(BF16)
-    rest = low - high_part.astype(F32)
-    mid_part = rest.astype(BF16)
-    low_part = (rest - mid_part.astype(F32)).astype(BF16)
-    tails = mm(flip, high_part) + (mm(flip, mid_part) + mm(flip, low_part))
+    turned = mm(reversal(reach), loads_ref[reach:]).astype(BF16)
+    tails = mm(mat_ref[:, reach:], loads_ref[0:reach]) + mm(mat_ref[:, 0:reach], turned)
     rhs = jnp.where(live_rows(size_ref, tails.shape), tails - decoded(heads_ref), 0.0)
     rhs_ref[...] = rhs
     rows = mm_wide((wt_hi[...], wt_lo[...]), rhs)
@@ -419,7 +414,7 @@
         + [pl.BlockSpec(memory_space=pltpu.VMEM)] * 5,
         name="rhs",
         compiler_params=GRANT,
-    )(size, nmat, load, heads, wt_hi, wt_lo)
+    )(size, n_own, load, heads, wt_hi, wt_lo)
 
     n_mats, d_mats = (n_own, n_away), (d_own, d_away)
     dual, dual_r = call(first_kernel, [field, rounded])(solve(payload, False), w_hi, w_lo)

time: 275 us -> 271 us (0.985)
  waiting for transfers between devices: 50.3 us -> 38.4 us
  starting transfers between devices: 46.6 us -> 57.1 us
    ppermute x13, starting transfers between devices: 13 us -> 24.3 us  [passed_along(): return lax.ppermute(block, SUB, [((i - distance) % n, i) for i in range(n)])]
    ppermute x3, waiting for transfers between devices: 17.5 us -> 7.05 us  [shards(): lax.ppermute(sent[d - 1], 'x', [(i, (i + d) % near) for i in range(near)])]
  transfers between devices with their start and end apart: 19 -> 19, of which waited for: 11 -> 12; matrix products, arithmetic and copies ran while one was open for 0% -> 1% of each run, Pallas kernels for 5% -> 5%
where the time goes in v3:
time: 271 us; the launch traced here: 270 us
  blocking collectives  136 us (50%)
  starting transfers between devices  57.1 us (21%)
  waiting for transfers between devices  38.4 us (14%)
  Pallas kernels  28.2 us (10%)
  local copies, waits for them, and re-layouts  7.52 us (3%)
    all_to_all x9, blocking collectives, exchange(): return lax.all_to_all(value, axes, 0, 0, tiled=True)  136 us
    all_to_all x3, starting transfers between devices, exchange(): return lax.all_to_all(value, axes, 0, 0, tiled=True)  28.7 us
    ppermute x13, starting transfers between devices, passed_along(): return lax.ppermute(block, SUB, [((i - distance) % n, i) for i in range(n)])  24.3 us
    ppermute x13, waiting for transfers between devices, passed_along(): return lax.ppermute(block, SUB, [((i - distance) % n, i) for i in range(n)])  16.7 us
    all_to_all x3, waiting for transfers between devices, exchange(): return lax.all_to_all(value, axes, 0, 0, tiled=True)  14.7 us
    unnamed x32, local copies, waits for them, and re-layouts  7.52 us
    ppermute x3, waiting for transfers between devices, shards(): lax.ppermute(sent[d - 1], 'x', [(i, (i + d) % near) for i in range(near)])  7.05 us
    pallas_call x5, Pallas kernels, apply(): pl.pallas_call(functools.partial(apply_kernel, mode), out_shape=[jax.Shap...  6.27 us
  transfers between devices with their start and end apart: 19, of which 12 were waited for; matrix products, arithmetic and copies ran while one was open for 1% of the time, Pallas kernels for 5%

profile of v3, /device:TPU:1, one launch (start us, length us, event | category | flops | bytes accessed | tf_op | source)
XLA Modules:
  0.0 269.8 jit_solution(2986543224472010591)
XLA Ops:
  0.6 1.6 copy-done.2
  2.2 1.0 copy-done.7
  3.8 3.3 %collective-permute-start.5 = (s16[528,256]{1,0:T(8,128)(2,1)S(1)}, s16[528,256]{1,0:T(8,128)(2,1)S(1)}, u32[]{:S(2)}, u32[]{:S(2)}) collective-permute-start(s16[528,256]{1,0:T(8,128)(2,1)S(1)} %shard_map.79), channel_id=1, source_target_pairs={{1,0},{2,1},{3,2},{4,3},{5,4},{6,5},{7,6},{8,7},{9,8},{10,9},{11,1... | collective-permute-start | bytes 811016 | tf_op jit(solution)/shard_map/ppermute | solution.py:320
  7.8 1.3 shard_map.77
  9.4 1.2 collective-permute-done.5.heads_ref
  10.6 2.0 rhs.1
  13.4 10.2 %all-to-all-start = ((s16[16,72,128]{2,1,0:T(8,128)(2,1)}), s16[16,72,128]{2,1,0:T(8,128)(2,1)}, u32[]{:S(2)}, u32[]{:S(2)}) async-start(s16[16,72,128]{2,1,0:T(8,128)(2,1)} %get-tuple-element.47), calls=%async_computation | async-start | bytes 589824 | tf_op jit(solution)/shard_map/all_to_all | solution.py:324
  24.5 4.0 %collective-permute-start.2 = (s16[144,512]{1,0:T(8,128)(2,1)S(1)}, s16[144,512]{1,0:T(8,128)(2,1)S(1)}, u32[]{:S(2)}, u32[]{:S(2)}) collective-permute-start(s16[144,512]{1,0:T(8,128)(2,1)S(1)} %get-tuple-element.43), channel_id=1, source_target_pairs={{0,4},{2,6},{4,0},{6,2},{1,5},{3,7},{5,1},{7,3},{8,12},{10,14},{12... | collective-permute-start | bytes 442376 | tf_op jit(solution)/shard_map/ppermute | solution.py:356
  28.5 1.7 collective-permute-done.1.refs_1_
  30.2 4.3 %collective-permute-done.2.refs_2_ = s16[144,512]{1,0:T(8,128)(2,1)S(1)} collective-permute-done((s16[144,512]{1,0:T(8,128)(2,1)S(1)}, s16[144,512]{1,0:T(8,128)(2,1)S(1)}, u32[]{:S(2)}, u32[]{:S(2)}) %collective-permute-start.2) | collective-permute-done | bytes 147488 | tf_op jit(solution)/shard_map/ppermute | solution.py:356
  34.6 1.0 collective-permute-done.3.refs_3_
  36.3 2.4 shard_map.80
  38.6 6.7 %all-to-all-start.1 = ((s16[16,72,128]{2,1,0:T(8,128)(2,1)}), s16[16,72,128]{2,1,0:T(8,128)(2,1)}, u32[]{:S(2)}, u32[]{:S(2)}) async-start(s16[16,72,128]{2,1,0:T(8,128)(2,1)} %shard_map.80), calls=%async_computation.1 | async-start | bytes 589824 | tf_op jit(solution)/shard_map/all_to_all | solution.py:324
  45.4 1.0 fusion
  46.4 6.8 %all-to-all-done.1.got_ref = s16[16,72,128]{2,1,0:T(8,128)(2,1)} async-done(((s16[16,72,128]{2,1,0:T(8,128)(2,1)}), s16[16,72,128]{2,1,0:T(8,128)(2,1)}, u32[]{:S(2)}, u32[]{:S(2)}) %all-to-all-start.1) | async-done | bytes 294944 | tf_op jit(solution)/shard_map/all_to_all | solution.py:324
  53.2 1.4 shard_map.81
  54.6 12.9 %collective-permute-start.7 = (bf16[512,256]{1,0:T(8,128)(2,1)S(1)}, bf16[512,256]{1,0:T(8,128)(2,1)S(1)}, u32[]{:S(2)}, u32[]{:S(2)}) collective-permute-start(bf16[512,256]{1,0:T(8,128)(2,1)S(1)} %get-tuple-element.48.xr_ref), channel_id=1, source_target_pairs={{1,0},{2,1},{3,2},{4,3},{5,4},{6,5},{7,6},{8,7},{9,8},{10,9},{11,1... | collective-permute-start | bytes 786440 | tf_op jit(solution)/shard_map/ppermute | solution.py:320
  68.2 3.5 %collective-permute-done.7.next_ref = bf16[512,256]{1,0:T(8,128)(2,1)S(1)} collective-permute-done((bf16[512,256]{1,0:T(8,128)(2,1)S(1)}, bf16[512,256]{1,0:T(8,128)(2,1)S(1)}, u32[]{:S(2)}, u32[]{:S(2)}) %collective-permute-start.7) | collective-permute-done | bytes 262176 | tf_op jit(solution)/shard_map/ppermute | solution.py:320
  71.8 0.8 shard_map.83
  74.1 11.8 %all-to-all-start.2 = ((s16[16,72,128]{2,1,0:T(8,128)(2,1)}), s16[16,72,128]{2,1,0:T(8,128)(2,1)}, u32[]{:S(2)}, u32[]{:S(2)}) async-start(s16[16,72,128]{2,1,0:T(8,128)(2,1)} %copy-done.12), calls=%async_computation.2 | async-start | bytes 589824 | tf_op jit(solution)/shard_map/all_to_all | solution.py:324
  86.0 1.6 copy-done.13
  87.5 2.3 shard_map.78
  89.8 1.0 copy-done
  90.9 7.4 %all-to-all-done.2.got_ref = s16[16,72,128]{2,1,0:T(8,128)(2,1)} async-done(((s16[16,72,128]{2,1,0:T(8,128)(2,1)}), s16[16,72,128]{2,1,0:T(8,128)(2,1)}, u32[]{:S(2)}, u32[]{:S(2)}) %all-to-all-start.2) | async-done | bytes 294944 | tf_op jit(solution)/shard_map/all_to_all | solution.py:324
  98.4 1.8 shard_map.84
  100.1 12.2 %all_to_all.60.got_ref = s16[16,72,128]{2,1,0:T(8,128)(2,1)S(1)} all-to-all(s16[16,72,128]{2,1,0:T(8,128)(2,1)S(1)} %shard_map.84), channel_id=1, replica_groups=mesh['grp'=4,'z'=8,'x'=4,'c'=2] {'grp','x'}, dimensions={0} | all-to-all | bytes 589824 | tf_op jit(solution)/shard_map/all_to_all | solution.py:324
  113.3 1.3 collective-permute-start.8
  114.6 1.7 shard_map.86.inner_ref
  116.2 2.4 collective-permute-done.9.next_ref
  118.6 2.1 shard_map.87
  120.7 23.0 %all_to_all.61.got_ref = s16[16,72,128]{2,1,0:T(8,128)(2,1)S(1)} all-to-all(s16[16,72,128]{2,1,0:T(8,128)(2,1)S(1)} %get-tuple-element.55), channel_id=1, replica_groups=mesh['grp'=4,'z'=8,'x'=4,'c'=2] {'z','c'}, dimensions={0} | all-to-all | bytes 589824 | tf_op jit(solution)/shard_map/all_to_all | solution.py:324
  144.4 12.7 %all_to_all.62.got_ref = s16[16,72,128]{2,1,0:T(8,128)(2,1)S(1)} all-to-all(s16[16,72,128]{2,1,0:T(8,128)(2,1)S(1)} %shard_map.88), channel_id=1, replica_groups=mesh['grp'=4,'z'=8,'x'=4,'c'=2] {'grp','x'}, dimensions={0} | all-to-all | bytes 589824 | tf_op jit(solution)/shard_map/all_to_all | solution.py:324
  157.6 1.1 collective-permute-start.11
  159.8 3.6 %collective-permute-done.11.next_ref = bf16[512,256]{1,0:T(8,128)(2,1)S(1)} collective-permute-done((bf16[512,256]{1,0:T(8,128)(2,1)S(1)}, bf16[512,256]{1,0:T(8,128)(2,1)S(1)}, u32[]{:S(2)}, u32[]{:S(2)}) %collective-permute-start.11) | collective-permute-done | bytes 262176 | tf_op jit(solution)/shard_map/ppermute | solution.py:320
  163.4 0.8 shard_map.91
  164.3 19.8 %all_to_all.63.got_ref = s16[16,72,128]{2,1,0:T(8,128)(2,1)S(1)} all-to-all(s16[16,72,128]{2,1,0:T(8,128)(2,1)S(1)} %get-tuple-element.59), channel_id=1, replica_groups=mesh['grp'=4,'z'=8,'x'=4,'c'=2] {'z','c'}, dimensions={0} | all-to-all | bytes 589824 | tf_op jit(solution)/shard_map/all_to_all | solution.py:324
  184.9 11.8 %all_to_all.64.got_ref = s16[16,72,128]{2,1,0:T(8,128)(2,1)S(1)} all-to-all(s16[16,72,128]{2,1,0:T(8,128)(2,1)S(1)} %shard_map.92), channel_id=1, replica_groups=mesh['grp'=4,'z'=8,'x'=4,'c'=2] {'grp','x'}, dimensions={0} | all-to-all | bytes 589824 | tf_op jit(solution)/shard_map/all_to_all | solution.py:324
  197.2 1.1 collective-permute-start.13
  199.0 1.7 shard_map.94.inner_ref
  200.7 2.4 collective-permute-done.13.next_ref
  203.1 2.1 shard_map.95
  205.1 19.7 %all_to_all.65.got_ref = s16[16,72,128]{2,1,0:T(8,128)(2,1)S(1)} all-to-all(s16[16,72,128]{2,1,0:T(8,128)(2,1)S(1)} %get-tuple-element.65), channel_id=1, replica_groups=mesh['grp'=4,'z'=8,'x'=4,'c'=2] {'z','c'}, dimensions={0} | all-to-all | bytes 589824 | tf_op jit(solution)/shard_map/all_to_all | solution.py:324
  225.6 11.8 %all_to_all.66.got_ref = s16[16,72,128]{2,1,0:T(8,128)(2,1)S(1)} all-to-all(s16[16,72,128]{2,1,0:T(8,128)(2,1)S(1)} %shard_map.96), channel_id=1, replica_groups=mesh['grp'=4,'z'=8,'x'=4,'c'=2] {'grp','x'}, dimensions={0} | all-to-all | bytes 589824 | tf_op jit(solution)/shard_map/all_to_all | solution.py:324
  237.8 1.1 collective-permute-start.15
  240.1 3.6 %collective-permute-done.15.next_ref = bf16[512,256]{1,0:T(8,128)(2,1)S(1)} collective-permute-done((bf16[512,256]{1,0:T(8,128)(2,1)S(1)}, bf16[512,256]{1,0:T(8,128)(2,1)S(1)}, u32[]{:S(2)}, u32[]{:S(2)}) %collective-permute-start.15) | collective-permute-done | bytes 262176 | tf_op jit(solution)/shard_map/ppermute | solution.py:320
  244.1 15.2 %all_to_all.67.got_ref = f32[16,8,128]{2,1,0:T(8,128)S(1)} all-to-all(f32[16,8,128]{2,1,0:T(8,128)S(1)} %get-tuple-element.69), channel_id=1, replica_groups=mesh['grp'=4,'z'=8,'x'=4,'c'=2] {'z','c'}, dimensions={0} | all-to-all | bytes 131072 | tf_op jit(solution)/shard_map/all_to_all | solution.py:324
  259.4 9.3 %all_to_all.68.got_ref = f32[16,8,128]{2,1,0:T(8,128)S(1)} all-to-all(f32[16,8,128]{2,1,0:T(8,128)S(1)} %shard_map.100), channel_id=1, replica_groups=mesh['grp'=4,'z'=8,'x'=4,'c'=2] {'grp','x'}, dimensions={0} | all-to-all | bytes 131072 | tf_op jit(solution)/shard_map/all_to_all | solution.py:324
  268.7 1.1 shard_map.101
  (65 shorter events, 13.7 us)
Async XLA Ops:
  0.6 7.1 %copy-start.15 = (s32[1,1,32]{2,1,0:T(1,128)S(1)}, s32[1,1,32]{2,1,0:T(1,128)}, u32[]{:S(2)}) copy-start(s32[1,1,32]{2,1,0:T(1,128)} %param.11) | copy-start | bytes 388
  0.6 1.6 copy-start.2
  2.2 1.0 copy-start.7
  3.8 6.8 %copy-start.8 = (bf16[1,1,1024,256]{3,2,1,0:T(8,128)(2,1)S(1)}, bf16[1,1,1024,256]{3,2,1,0:T(8,128)(2,1)}, u32[]{:S(2)}) copy-start(bf16[1,1,1024,256]{3,2,1,0:T(8,128)(2,1)} %param.9) | copy-start | bytes 1572868
  3.8 6.8 %collective-permute-start.5 = (s16[528,256]{1,0:T(8,128)(2,1)S(1)}, s16[528,256]{1,0:T(8,128)(2,1)S(1)}, u32[]{:S(2)}, u32[]{:S(2)}) collective-permute-start(s16[528,256]{1,0:T(8,128)(2,1)S(1)} %shard_map.79), channel_id=1, source_target_pairs={{1,0},{2,1},{3,2},{4,3},{5,4},{6,5},{7,6},{8,7},{9,8},{10,9},{11,1... | collective-permute-start | bytes 811016 | tf_op jit(solution)/shard_map/ppermute | solution.py:320
  7.8 16.1 %copy-start.9 = (f32[1,1,128,2048]{3,2,1,0:T(8,128)S(1)}, f32[1,1,128,2048]{3,2,1,0:T(8,128)}, u32[]{:S(2)}) copy-start(f32[1,1,128,2048]{3,2,1,0:T(8,128)} %param.8) | copy-start | bytes 3145732
  9.1 3.5 %copy-start.14 = (bf16[512,1024]{1,0:T(8,128)(2,1)}, bf16[512,1024]{1,0:T(8,128)(2,1)S(1)}, u32[]{:S(2)}) copy-start(bf16[512,1024]{1,0:T(8,128)(2,1)S(1)} %get-tuple-element.40) | copy-start | bytes 3145732
  12.6 0.8 copy-start.10
  13.4 22.9 %all-to-all-start = ((s16[16,72,128]{2,1,0:T(8,128)(2,1)}), s16[16,72,128]{2,1,0:T(8,128)(2,1)}, u32[]{:S(2)}, u32[]{:S(2)}) async-start(s16[16,72,128]{2,1,0:T(8,128)(2,1)} %get-tuple-element.47), calls=%async_computation | async-start | bytes 589824 | tf_op jit(solution)/shard_map/all_to_all | solution.py:324
  23.6 44.2 %collective-permute-start = (bf16[512,1024]{1,0:T(8,128)(2,1)}, bf16[512,1024]{1,0:T(8,128)(2,1)S(1)}, u32[]{:S(2)}, u32[]{:S(2)}) collective-permute-start(bf16[512,1024]{1,0:T(8,128)(2,1)} %copy-done.14), channel_id=1, source_target_pairs={{1,0},{2,1},{3,2},{4,3},{5,4},{6,5},{7,6},{8,7},{9,8},{10,9},{11,1... | collective-permute-start | bytes 3145736 | tf_op jit(solution)/shard_map/ppermute | solution.py:320
  24.4 5.9 %collective-permute-start.1 = (s16[144,512]{1,0:T(8,128)(2,1)S(1)}, s16[144,512]{1,0:T(8,128)(2,1)S(1)}, u32[]{:S(2)}, u32[]{:S(2)}) collective-permute-start(s16[144,512]{1,0:T(8,128)(2,1)S(1)} %get-tuple-element.42), channel_id=1, source_target_pairs={{0,2},{2,4},{4,6},{6,0},{1,3},{3,5},{5,7},{7,1},{8,10},{10,12},{12... | collective-permute-start | bytes 442376 | tf_op jit(solution)/shard_map/ppermute | solution.py:356
  24.5 10.1 %collective-permute-start.2 = (s16[144,512]{1,0:T(8,128)(2,1)S(1)}, s16[144,512]{1,0:T(8,128)(2,1)S(1)}, u32[]{:S(2)}, u32[]{:S(2)}) collective-permute-start(s16[144,512]{1,0:T(8,128)(2,1)S(1)} %get-tuple-element.43), channel_id=1, source_target_pairs={{0,4},{2,6},{4,0},{6,2},{1,5},{3,7},{5,1},{7,3},{8,12},{10,14},{12... | collective-permute-start | bytes 442376 | tf_op jit(solution)/shard_map/ppermute | solution.py:356
  28.5 7.1 %collective-permute-start.3 = (s16[144,512]{1,0:T(8,128)(2,1)S(1)}, s16[144,512]{1,0:T(8,128)(2,1)S(1)}, u32[]{:S(2)}, u32[]{:S(2)}) collective-permute-start(s16[144,512]{1,0:T(8,128)(2,1)S(1)} %get-tuple-element.44), channel_id=1, source_target_pairs={{0,6},{2,0},{4,2},{6,4},{1,7},{3,1},{5,3},{7,5},{8,14},{10,8},{12,... | collective-permute-start | bytes 442376 | tf_op jit(solution)/shard_map/ppermute | solution.py:356
  38.6 14.5 %all-to-all-start.1 = ((s16[16,72,128]{2,1,0:T(8,128)(2,1)}), s16[16,72,128]{2,1,0:T(8,128)(2,1)}, u32[]{:S(2)}, u32[]{:S(2)}) async-start(s16[16,72,128]{2,1,0:T(8,128)(2,1)} %shard_map.80), calls=%async_computation.1 | async-start | bytes 589824 | tf_op jit(solution)/shard_map/all_to_all | solution.py:324
  53.2 18.6 %copy-start.11 = (f32[512,256]{1,0:T(8,128)S(1)}, f32[512,256]{1,0:T(8,128)}, u32[]{:S(2)}) copy-start(f32[512,256]{1,0:T(8,128)} %copy-done.10) | copy-start | bytes 1572868
  54.6 18.0 %copy-start.3 = (f32[512,256]{1,0:T(8,128)}, f32[512,256]{1,0:T(8,128)S(1)}, u32[]{:S(2)}) copy-start(f32[512,256]{1,0:T(8,128)S(1)} %get-tuple-element.49.x_ref.dual_ref) | copy-start | bytes 1572868
  54.6 17.1 %collective-permute-start.7 = (bf16[512,256]{1,0:T(8,128)(2,1)S(1)}, bf16[512,256]{1,0:T(8,128)(2,1)S(1)}, u32[]{:S(2)}, u32[]{:S(2)}) collective-permute-start(bf16[512,256]{1,0:T(8,128)(2,1)S(1)} %get-tuple-element.48.xr_ref), channel_id=1, source_target_pairs={{1,0},{2,1},{3,2},{4,3},{5,4},{6,5},{7,6},{8,7},{9,8},{10,9},{11,1... | collective-permute-start | bytes 786440 | tf_op jit(solution)/shard_map/ppermute | solution.py:320
  67.5 4.2 %collective-permute-start.6 = (bf16[512,256]{1,0:T(8,128)(2,1)S(1)}, bf16[512,256]{1,0:T(8,128)(2,1)S(1)}, u32[]{:S(2)}, u32[]{:S(2)}) collective-permute-start(bf16[512,256]{1,0:T(8,128)(2,1)S(1)} %get-tuple-element.48.xr_ref), channel_id=1, source_target_pairs={{63,0},{0,1},{1,2},{2,3},{3,4},{4,5},{5,6},{6,7},{7,8},{8,9},{9,10... | collective-permute-start | bytes 786440 | tf_op jit(solution)/shard_map/ppermute | solution.py:320
  72.6 0.8 copy-start.5
  73.4 0.7 copy-start.12
  74.1 24.2 %all-to-all-start.2 = ((s16[16,72,128]{2,1,0:T(8,128)(2,1)}), s16[16,72,128]{2,1,0:T(8,128)(2,1)}, u32[]{:S(2)}, u32[]{:S(2)}) async-start(s16[16,72,128]{2,1,0:T(8,128)(2,1)} %copy-done.12), calls=%async_computation.2 | async-start | bytes 589824 | tf_op jit(solution)/shard_map/all_to_all | solution.py:324
  86.0 1.6 copy-start.13
  89.8 1.0 copy-start
  90.8 23.8 %collective-permute-start.4 = (bf16[512,1024]{1,0:T(8,128)(2,1)}, bf16[512,1024]{1,0:T(8,128)(2,1)}, u32[]{:S(2)}, u32[]{:S(2)}) collective-permute-start(bf16[512,1024]{1,0:T(8,128)(2,1)} %get-tuple-element.46), channel_id=1, source_target_pairs={{1,0},{2,1},{3,2},{4,3},{5,4},{6,5},{7,6},{8,7},{9,8},{10,9},{11,1... | collective-permute-start | bytes 3145736 | tf_op jit(solution)/shard_map/ppermute | solution.py:320
  98.3 14.0 %copy-start.6 = (f32[512,256]{1,0:T(8,128)S(1)}, f32[512,256]{1,0:T(8,128)}, u32[]{:S(2)}) copy-start(f32[512,256]{1,0:T(8,128)} %copy-done.5) | copy-start | bytes 1572868
  98.4 16.2 %copy-start.1 = (bf16[512,1024]{1,0:T(8,128)(2,1)S(1)}, bf16[512,1024]{1,0:T(8,128)(2,1)}, u32[]{:S(2)}) copy-start(bf16[512,1024]{1,0:T(8,128)(2,1)} %copy-done) | copy-start | bytes 3145732
  112.7 5.9 %collective-permute-start.9 = (bf16[512,256]{1,0:T(8,128)(2,1)S(1)}, bf16[512,256]{1,0:T(8,128)(2,1)S(1)}, u32[]{:S(2)}, u32[]{:S(2)}) collective-permute-start(bf16[512,256]{1,0:T(8,128)(2,1)S(1)} %get-tuple-element.53.xr_ref), channel_id=1, source_target_pairs={{1,0},{2,1},{3,2},{4,3},{5,4},{6,5},{7,6},{8,7},{9,8},{10,9},{11,1... | collective-permute-start | bytes 786440 | tf_op jit(solution)/shard_map/ppermute | solution.py:320
  113.3 5.4 %collective-permute-start.8 = (bf16[512,256]{1,0:T(8,128)(2,1)S(1)}, bf16[512,256]{1,0:T(8,128)(2,1)S(1)}, u32[]{:S(2)}, u32[]{:S(2)}) collective-permute-start(bf16[512,256]{1,0:T(8,128)(2,1)S(1)} %get-tuple-element.53.xr_ref), channel_id=1, source_target_pairs={{63,0},{0,1},{1,2},{2,3},{3,4},{4,5},{5,6},{6,7},{7,8},{8,9},{9,10... | collective-permute-start | bytes 786440 | tf_op jit(solution)/shard_map/ppermute | solution.py:320
  157.6 5.9 %collective-permute-start.11 = (bf16[512,256]{1,0:T(8,128)(2,1)S(1)}, bf16[512,256]{1,0:T(8,128)(2,1)S(1)}, u32[]{:S(2)}, u32[]{:S(2)}) collective-permute-start(bf16[512,256]{1,0:T(8,128)(2,1)S(1)} %get-tuple-element.57.xr_ref), channel_id=1, source_target_pairs={{1,0},{2,1},{3,2},{4,3},{5,4},{6,5},{7,6},{8,7},{9,8},{10,9},{11,1... | collective-permute-start | bytes 786440 | tf_op jit(solution)/shard_map/ppermute | solution.py:320
  158.7 4.8 %collective-permute-start.10 = (bf16[512,256]{1,0:T(8,128)(2,1)S(1)}, bf16[512,256]{1,0:T(8,128)(2,1)S(1)}, u32[]{:S(2)}, u32[]{:S(2)}) collective-permute-start(bf16[512,256]{1,0:T(8,128)(2,1)S(1)} %get-tuple-element.57.xr_ref), channel_id=1, source_target_pairs={{63,0},{0,1},{1,2},{2,3},{3,4},{4,5},{5,6},{6,7},{7,8},{8,9},{9,10... | collective-permute-start | bytes 786440 | tf_op jit(solution)/shard_map/ppermute | solution.py:320
  164.3 32.4 %copy-start.4 = (f32[512,256]{1,0:T(8,128)S(1)}, f32[512,256]{1,0:T(8,128)}, u32[]{:S(2)}) copy-start(f32[512,256]{1,0:T(8,128)} %copy-done.3) | copy-start | bytes 1572868
  197.2 5.9 %collective-permute-start.13 = (bf16[512,256]{1,0:T(8,128)(2,1)S(1)}, bf16[512,256]{1,0:T(8,128)(2,1)S(1)}, u32[]{:S(2)}, u32[]{:S(2)}) collective-permute-start(bf16[512,256]{1,0:T(8,128)(2,1)S(1)} %get-tuple-element.63.xr_ref), channel_id=1, source_target_pairs={{1,0},{2,1},{3,2},{4,3},{5,4},{6,5},{7,6},{8,7},{9,8},{10,9},{11,1... | collective-permute-start | bytes 786440 | tf_op jit(solution)/shard_map/ppermute | solution.py:320
  198.3 4.8 %collective-permute-start.12 = (bf16[512,256]{1,0:T(8,128)(2,1)S(1)}, bf16[512,256]{1,0:T(8,128)(2,1)S(1)}, u32[]{:S(2)}, u32[]{:S(2)}) collective-permute-start(bf16[512,256]{1,0:T(8,128)(2,1)S(1)} %get-tuple-element.63.xr_ref), channel_id=1, source_target_pairs={{63,0},{0,1},{1,2},{2,3},{3,4},{4,5},{5,6},{6,7},{7,8},{8,9},{9,10... | collective-permute-start | bytes 786440 | tf_op jit(solution)/shard_map/ppermute | solution.py:320
  237.8 5.9 %collective-permute-start.15 = (bf16[512,256]{1,0:T(8,128)(2,1)S(1)}, bf16[512,256]{1,0:T(8,128)(2,1)S(1)}, u32[]{:S(2)}, u32[]{:S(2)}) collective-permute-start(bf16[512,256]{1,0:T(8,128)(2,1)S(1)} %get-tuple-element.67.xr_ref), channel_id=1, source_target_pairs={{1,0},{2,1},{3,2},{4,3},{5,4},{6,5},{7,6},{8,7},{9,8},{10,9},{11,1... | collective-permute-start | bytes 786440 | tf_op jit(solution)/shard_map/ppermute | solution.py:320
  238.9 4.8 %collective-permute-start.14 = (bf16[512,256]{1,0:T(8,128)(2,1)S(1)}, bf16[512,256]{1,0:T(8,128)(2,1)S(1)}, u32[]{:S(2)}, u32[]{:S(2)}) collective-permute-start(bf16[512,256]{1,0:T(8,128)(2,1)S(1)} %get-tuple-element.67.xr_ref), channel_id=1, source_target_pairs={{63,0},{0,1},{1,2},{2,3},{3,4},{4,5},{5,6},{6,7},{7,8},{8,9},{9,10... | collective-permute-start | bytes 786440 | tf_op jit(solution)/shard_map/ppermute | solution.py:320
